TPU v7x, 32 devices: a whole 2x2x4 slice. The times are simulated.
32 devices in a mesh: grp: 4 (over y, core), tm: 8 (over z, x).
Axes of the slice: x: 2, y: 2, z: 4, core: 2. Of those that a mesh axis runs over, the one named last changes fastest.
Arguments:
- wave: bfloat16 [4, 327680], P('grp', 'tm'), may hold values from -6 to 6
- assign: int32 [4, 1024], P('grp', 'tm'), may hold values from 0 to 16383
- w_first: bfloat16 [10, 512], replicated, may hold values from -2 to 2
- w_mid: bfloat16 [4, 1536, 512], replicated, may hold values from -0.15625 to 0.15625
- w_tail: bfloat16 [2, 1024, 512], replicated, may hold values from -0.1875 to 0.1875
- w_proj: bfloat16 [512, 768], replicated, may hold values from -0.25 to 0.25
- centroids: float32 [16384, 768], P('tm'), may hold values from -6 to 6
- prior: float32 [16384], P('tm'), may hold values from 1 to 16
Outputs:
- new_centroids: float32 [16384, 768], P('tm')
- new_counts: float32 [16384], P('tm')
- distortion: float32 [4, 1024], P('grp', 'tm')
All inputs are finite; a program needn't handle non-finite values.
Results may differ from a plain program's by a relative error of at most 0.007.
Values may be sent and summed in bfloat16 or wider, within the bound.
A program may use at most 128 MiB of HBM per device.

v0:
```python
import jax
import jax.numpy as jnp
from jax import lax
from jax.sharding import PartitionSpec as P

HALO = 80


EPS = 1e-05


def passed_along(value, axis, steps):
    count = lax.axis_size(axis)
    leading, last = (max(0, -steps), min(count, count - steps))
    return lax.ppermute(value, axis, [(source, source + steps) for source in range(leading, last)])


def norm_rows(accum):
    row_mean = jnp.mean(accum, axis=-1, keepdims=True)
    centred = accum - row_mean
    spread = jnp.mean(centred * centred, axis=-1, keepdims=True)
    return centred * lax.rsqrt(spread + EPS)


def activate(accum):
    return jax.nn.gelu(norm_rows(accum), approximate=False).astype(jnp.bfloat16)


def first_layer(samples, w_first):
    windows = samples.reshape(-1, 5)
    accum = jnp.dot(windows[:-1], w_first[:5], preferred_element_type=jnp.float32)
    accum = accum + jnp.dot(windows[1:], w_first[5:], preferred_element_type=jnp.float32)
    return activate(accum)


def odd_layer(inputs, weight):
    channels = inputs.shape[1]
    out_len = (inputs.shape[0] - 3) // 2 + 1
    paired = jnp.concatenate([inputs, jnp.zeros((1, channels), inputs.dtype)], axis=0).reshape(
        out_len + 1, 2 * channels
    )
    accum = jnp.dot(paired[:out_len], weight[: 2 * channels], preferred_element_type=jnp.float32)
    accum = accum + jnp.dot(
        paired[1:, :channels], weight[2 * channels :], preferred_element_type=jnp.float32
    )
    return activate(accum)


def even_layer(inputs, weight):
    channels = inputs.shape[1]
    paired = inputs.reshape(inputs.shape[0] // 2, 2 * channels)
    return activate(jnp.dot(paired, weight, preferred_element_type=jnp.float32))


def encode(samples, w_first, w_mid, w_tail):
    hidden = first_layer(samples, w_first)
    for layer_num in range(4):
        hidden = odd_layer(hidden, w_mid[layer_num])
    for layer_num in range(2):
        hidden = even_layer(hidden, w_tail[layer_num])
    return hidden


def project(features, w_proj):
    normed = norm_rows(features.astype(jnp.float32)).astype(jnp.bfloat16)
    return jnp.dot(normed, w_proj, preferred_element_type=jnp.float32).astype(jnp.bfloat16)


def local(wave, assign, w_first, w_mid, w_tail, w_proj, centroids, prior):
    samples = wave[0]
    tail_part = passed_along(samples[:HALO], "tm", -1)
    features = encode(jnp.concatenate([samples, tail_part]), w_first, w_mid, w_tail)
    own_labels = assign[0]
    shard_len = centroids.shape[0]
    feat_width = centroids.shape[1]
    first_id = lax.axis_index("tm") * shard_len
    centroid_ids = first_id + jnp.arange(shard_len, dtype=jnp.int32)
    rounded = lax.optimization_barrier(centroids.astype(jnp.bfloat16))
    widened = rounded.astype(jnp.float32)
    centroid_sq = jnp.sum(widened * widened, axis=1)
    frames = project(features, w_proj)
    accumulate_frames = lax.all_gather(frames, "tm", axis=0, tiled=True)
    labels = lax.all_gather(own_labels, "tm", axis=0, tiled=True)
    one_hot = labels[None, :] == centroid_ids[:, None]
    hot_rows = labels[:, None] == centroid_ids[None, :]
    hot_sums = jnp.dot(
        one_hot.astype(jnp.bfloat16), accumulate_frames, preferred_element_type=jnp.float32
    )
    counts = jnp.sum(one_hot.astype(jnp.float32), axis=1)
    products = jnp.einsum(
        "rd,kd->rk", accumulate_frames, rounded, preferred_element_type=jnp.float32
    )
    frame_wide = accumulate_frames.astype(jnp.float32)
    squares = jnp.sum(frame_wide * frame_wide, axis=1)
    is_owner = (labels >= first_id) & (labels < first_id + shard_len)
    picked = jnp.sum(jnp.where(hot_rows, centroid_sq[None, :] - 2.0 * products, 0.0), axis=1)
    own_term = jnp.where(is_owner, squares + picked, 0.0)
    term_sums = lax.psum_scatter(own_term, "tm", scatter_dimension=0, tiled=True)
    distortion = (term_sums / feat_width)[None, :]
    total_sums, total_counts = (
        lax.psum(hot_sums.astype(jnp.bfloat16), "grp").astype(jnp.float32),
        lax.psum(counts.astype(jnp.bfloat16), "grp").astype(jnp.float32),
    )
    new_counts = prior + total_counts
    new_centroids = (prior[:, None] * centroids + total_sums) / new_counts[:, None]
    return (new_centroids, new_counts, distortion)


def solution(mesh):
    return jax.shard_map(
        local,
        mesh=mesh,
        in_specs=(P("grp", "tm"), P("grp", "tm"), P(), P(), P(), P(), P("tm", None), P("tm")),
        out_specs=(P("tm", None), P("tm"), P("grp", "tm")),
        check_vma=False,
    )
```

profile of v0, /device:TPU:0, one launch (start us, length us, event | category | flops | bytes accessed | tf_op | source)
XLA Modules:
  0.0 410.7 jit_solution(17534476603627418723)
XLA Ops:
  8.0 1.3 collective-permute-start
  9.2 1.4 reduce
  10.6 3.7 collective-permute-done
  14.4 4.5 %slice.152 = bf16[8207,5]{1,0:T(8,128)(2,1)S(1)} reshape(bf16[41035]{0:T(1024)(128)(2,1)S(1)} %get-tuple-element.8) | data formatting | bytes 164140 | tf_op jit(solution)/shard_map/slice | solution.py:32
  19.0 5.9 %slice.149 = bf16[8207,5]{1,0:T(8,128)(2,1)} reshape(bf16[41035]{0:T(1024)(128)(2,1)S(1)} %get-tuple-element.7) | data formatting | bytes 164140 | tf_op jit(solution)/shard_map/slice | solution.py:31
  24.8 8.0 %fusion.115 = f32[8207,512]{1,0:T(8,128)} fusion(bf16[8207,5]{1,0:T(8,128)(2,1)S(1)} %slice.152, bf16[10,512]{1,0:T(8,128)(2,1)S(1)} %copy-done.9), kind=kOutput, calls=%fused_computation.204 | convolution fusion | flops 42019840 | bytes 18917376 | tf_op jit(solution)/shard_map/dot_general | solution.py:32
  32.9 11.1 %fusion.121 = (f32[8207]{0:T(1024)S(1)}, f32[8207,512]{1,0:T(8,128)}) fusion(f32[8207,512]{1,0:T(8,128)} %fusion.115, bf16[8207,5]{1,0:T(8,128)(2,1)S(1)} %copy-done.5, bf16[10,512]{1,0:T(8,128)(2,1)S(1)} %copy-done.9), kind=kOutput, calls=%fused_computation.223 | convolution fusion | flops 50415600 | bytes 35758140 | tf_op jit(solution)/shard_map/dot_general | solution.py:31
  44.0 10.4 %multiply_reduce_fusion = f32[8207]{0:T(1024)S(1)} fusion(f32[8207,512]{1,0:T(8,128)} %get-tuple-element.10, f32[8207]{0:T(1024)S(1)} %broadcast_multiply_fusion), kind=kLoop, calls=%fused_computation.17 | loop fusion | flops 12597745 | bytes 16873592 | tf_op jit(solution)/shard_map/reduce_sum | solution.py:21
  54.7 45.7 %fusion.2 = bf16[8207,512]{1,0:T(8,128)(2,1)} fusion(f32[8207,512]{1,0:T(8,128)S(1)} %copy-done.1, f32[8207]{0:T(1024)S(1)} %add_rsqrt_fusion, f32[8207]{0:T(1024)S(1)} %broadcast_multiply_fusion), kind=kLoop, calls=%fused_computation.3 | loop fusion | flops 281532928 | bytes 25277560 | tf_op jit(solution)/shard_map/convert_element_type | solution.py:26
  100.4 13.0 %slice.155 = bf16[4103,1024]{1,0:T(8,128)(2,1)} reshape(bf16[8206,512]{1,0:T(8,128)(2,1)} %bitcast.63) | data formatting | bytes 16805888 | tf_op jit(solution)/shard_map/slice | solution.py:42
  113.4 8.0 %concatenate.16 = bf16[8208,512]{1,0:T(8,128)(2,1)} pad(bf16[8207,512]{1,0:T(8,128)(2,1)} %fusion.2, bf16[]{:T(256)} %constant.70.clone.1), padding=0_1x0_0 | pad | bytes 16808962 | tf_op jit(solution)/shard_map/concatenate | solution.py:39
  121.4 13.0 %reshape.165 = bf16[4104,1024]{1,0:T(8,128)(2,1)} reshape(bf16[8208,512]{1,0:T(8,128)(2,1)} %concatenate.16) | data formatting | bytes 16809984 | tf_op jit(solution)/shard_map/reshape | solution.py:39
  134.4 7.4 %fusion.64 = f32[4103,512]{1,0:T(8,128)S(1)} fusion(bf16[4103,1024]{1,0:T(8,128)(2,1)} %slice.155, bf16[4,1536,512]{2,1,0:T(8,128)(2,1)} %param.11), kind=kOutput, calls=%fused_computation.114 | convolution fusion | flops 4302307328 | bytes 17856512 | tf_op jit(solution)/shard_map/dot_general | solution.py:42
  141.9 3.7 fusion.122
  145.6 1.7 multiply_reduce_fusion.1
  147.3 22.3 %fusion.14 = bf16[4103,512]{1,0:T(8,128)(2,1)S(1)} fusion(f32[4103,512]{1,0:T(8,128)S(1)} %get-tuple-element.12, f32[4103]{0:T(1024)S(1)} %add_rsqrt_fusion.1, f32[4103]{0:T(1024)S(1)} %broadcast_multiply_fusion.1), kind=kLoop, calls=%fused_computation.27 | loop fusion | flops 140749312 | bytes 12637240 | tf_op jit(solution)/shard_map/convert_element_type | solution.py:26
  169.6 1.9 copy-done.2
  171.6 2.2 concatenate.17
  173.8 7.2 %slice.162 = bf16[2051,1024]{1,0:T(8,128)(2,1)} reshape(bf16[4102,512]{1,0:T(8,128)(2,1)} %bitcast.64) | data formatting | bytes 8400896 | tf_op jit(solution)/shard_map/slice | solution.py:42
  181.0 6.8 %fusion.62 = f32[2051,512]{1,0:T(8,128)} fusion(bf16[2051,1024]{1,0:T(8,128)(2,1)} %slice.162, bf16[4,1536,512]{2,1,0:T(8,128)(2,1)} %param.11), kind=kOutput, calls=%fused_computation.112 | convolution fusion | flops 2150629376 | bytes 9459712 | tf_op jit(solution)/shard_map/dot_general | solution.py:42
  187.8 7.2 %reshape.166 = bf16[2052,1024]{1,0:T(8,128)(2,1)} reshape(bf16[4104,512]{1,0:T(8,128)(2,1)} %concatenate.17) | data formatting | bytes 8404992 | tf_op jit(solution)/shard_map/reshape | solution.py:39
  194.9 4.5 %fusion.123 = (f32[2051]{0:T(1024)S(1)}, f32[2051,512]{1,0:T(8,128)S(1)}) fusion(f32[2051,512]{1,0:T(8,128)} %fusion.62, bf16[4,1536,512]{2,1,0:T(8,128)(2,1)} %param.11, bf16[2052,1024]{1,0:T(8,128)(2,1)} %reshape.166), kind=kOutput, calls=%fused_computation.225 | convolution fusion | flops 1077412864 | bytes 11048972 | tf_op jit(solution)/shard_map/dot_general | solution.py:43
  199.4 0.9 multiply_reduce_fusion.3
  200.3 11.5 %fusion.25 = bf16[2051,512]{1,0:T(8,128)(2,1)S(1)} fusion(f32[2051,512]{1,0:T(8,128)S(1)} %get-tuple-element.14, f32[2051]{0:T(1024)S(1)} %add_rsqrt_fusion.2, f32[2051]{0:T(1024)S(1)} %broadcast_multiply_fusion.2), kind=kLoop, calls=%fused_computation.53 | loop fusion | flops 70357504 | bytes 6317080 | tf_op jit(solution)/shard_map/convert_element_type | solution.py:26
  211.9 1.4 concatenate.18
  213.3 2.0 slice.169
  215.3 4.6 %fusion.60 = f32[1025,512]{1,0:T(8,128)} fusion(bf16[1025,1024]{1,0:T(8,128)(2,1)} %slice.169, bf16[4,1536,512]{2,1,0:T(8,128)(2,1)} %param.11), kind=kOutput, calls=%fused_computation.110 | convolution fusion | flops 1074790400 | bytes 5261312 | tf_op jit(solution)/shard_map/dot_general | solution.py:42
  220.0 2.0 reshape.167
  222.0 2.9 fusion.124
  225.4 5.7 %fusion.41 = bf16[1025,512]{1,0:T(8,128)(2,1)S(1)} fusion(f32[1025,512]{1,0:T(8,128)S(1)} %get-tuple-element.16, f32[1025]{0:T(1024)S(1)} %add_rsqrt_fusion.3, f32[1025]{0:T(1024)S(1)} %broadcast_multiply_fusion.3), kind=kLoop, calls=%fused_computation.79 | loop fusion | flops 35161600 | bytes 3157000 | tf_op jit(solution)/shard_map/convert_element_type | solution.py:26
  231.2 1.2 slice.176
  232.4 3.3 fusion.58
  236.0 1.9 fusion.125
  238.1 2.6 fusion.53
  241.2 1.7 fusion.126
  243.2 1.3 fusion.81
  244.6 1.6 fusion.127
  246.4 0.8 convert_reduce_fusion
  247.4 1.0 convolution_convert_fusion
  248.5 19.6 %all-gather = s32[1,1024]{1,0:T(1,128)S(1)} all-gather(s32[1,128]{1,0:T(1,128)S(1)} %copy-done.10), channel_id=2, replica_groups=mesh['grp'=4,'tm'=8] {'tm'}, dimensions={1}, use_global_device_ids=true | all-gather | bytes 4608 | tf_op jit(solution)/shard_map/all_gather | solution.py:83
  268.0 26.3 %all-gather.3.cloned.1.call-done = bf16[1024,768]{1,0:T(8,128)(2,1)} async-done(((bf16[128,768]{1,0:T(8,128)(2,1)}), bf16[1024,768]{1,0:T(8,128)(2,1)}) %all-gather.3.cloned.1.call-update) | async-done | bytes 1572880 | tf_op jit(solution)/shard_map/all_gather | solution.py:82
  294.4 6.3 %fusion.36 = bf16[2048,768]{1,0:T(8,128)(2,1)} fusion(bf16[1024,768]{1,0:T(8,128)(2,1)} %all-gather.3.cloned.1.call-done, s32[1024]{0:T(1024)S(1)} %bitcast.66, s32[2048]{0:T(1024)S(1)} %iota_add_fusion), kind=kOutput, calls=%fused_computation.74 | convolution fusion | flops 3224895488 | bytes 4730880 | tf_op jit(solution)/shard_map/dot_general | solution.py:86
  302.0 1.1 fusion.22
  303.1 6.4 %psum.15 = bf16[2048]{0:T(1024)(128)(2,1)S(1)} all-reduce(bf16[2048]{0:T(1024)(128)(2,1)S(1)} %fusion.22), channel_id=1, replica_groups=mesh['grp'=4,'tm'=8] {'grp'}, use_global_device_ids=true, to_apply=%region_18.0 | all-reduce | flops 2048 | bytes 8192 | tf_op jit(solution)/shard_map/psum | solution.py:102
  310.0 58.2 %all-reduce.7.cloned.1.call-done = bf16[2048,768]{1,0:T(8,128)(2,1)} async-done(((bf16[2048,768]{1,0:T(8,128)(2,1)}), bf16[2048,768]{1,0:T(8,128)(2,1)}) %all-reduce.7.cloned.1.call-update) | async-done | bytes 3145744 | tf_op jit(solution)/shard_map/psum | solution.py:101
  368.2 8.7 %fusion.120 = (bf16[2048,768]{1,0:T(8,128)(2,1)S(1)}, f32[2048,768]{1,0:T(8,128)}) fusion(f32[2048,768]{1,0:T(8,128)} %param.14, f32[2048]{0:T(1024)S(1)} %convert_add_fusion, bf16[2048,768]{1,0:T(8,128)(2,1)} %all-reduce.7.cloned.1.call-done, f32[2048]{0:T(1024)S(1)} %copy-done.7), kind=kLoop, calls=%fused_computation.222 | loop fusion | flops 7864320 | bytes 18890752 | tf_op jit(solution)/shard_map/convert_element_type | solution.py:78
  377.6 4.0 select_reduce_fusion
  381.6 21.4 %all-reduce.4 = f32[1024]{0:T(1024)S(1)} all-reduce(f32[1024]{0:T(1024)S(1)} %add_select_fusion), channel_id=3, replica_groups=mesh['grp'=4,'tm'=8] {'tm'}, use_global_device_ids=true, to_apply=%region_22.23.clone | all-reduce | flops 1024 | bytes 8192
  (63 shorter events, 5.8 us)
Async XLA Ops:
  7.2 240.2 %copy-start = (bf16[512,768]{1,0:T(8,128)(2,1)S(1)}, bf16[512,768]{1,0:T(8,128)(2,1)}, u32[]{:S(2)}) copy-start(bf16[512,768]{1,0:T(8,128)(2,1)} %param.13) | copy-start | bytes 2359300
  7.2 17.6 %copy-start.9 = (bf16[10,512]{1,0:T(8,128)(2,1)S(1)}, bf16[10,512]{1,0:T(8,128)(2,1)}, u32[]{:S(2)}) copy-start(bf16[10,512]{1,0:T(8,128)(2,1)} %param.10) | copy-start | bytes 30724
  7.2 287.2 %all-gather.3.cloned.1.call-start = ((), (), s32[]{:S(2)}) async-start(), calls=%async_computation | async-start | bytes 1769472 | tf_op jit(solution)/shard_map/all_gather | solution.py:82
  8.0 6.3 %collective-permute-start = (bf16[80]{0:T(256)(128)(2,1)S(1)}, bf16[80]{0:T(256)(128)(2,1)S(1)}, u32[]{:S(2)}, u32[]{:S(2)}) collective-permute-start(bf16[80]{0:T(256)(128)(2,1)S(1)} %slice_bitcast_fusion), channel_id=1, source_target_pairs={{1,0},{2,1},{3,2},{4,3},{5,4},{6,5},{7,6},{9,8},{10,9},{11,10},{12... | collective-permute-start | bytes 488 | tf_op jit(solution)/shard_map/ppermute | solution.py:15
  24.8 8.0 %copy-start.5 = (bf16[8207,5]{1,0:T(8,128)(2,1)S(1)}, bf16[8207,5]{1,0:T(8,128)(2,1)}, u32[]{:S(2)}) copy-start(bf16[8207,5]{1,0:T(8,128)(2,1)} %slice.149) | copy-start | bytes 246214
  44.0 10.7 %copy-start.1 = (f32[8207,512]{1,0:T(8,128)S(1)}, f32[8207,512]{1,0:T(8,128)}, u32[]{:S(2)}) copy-start(f32[8207,512]{1,0:T(8,128)} %get-tuple-element.10) | copy-start | bytes 50423812
  134.4 7.4 %copy-start.3 = (bf16[4104,1024]{1,0:T(8,128)(2,1)S(1)}, bf16[4104,1024]{1,0:T(8,128)(2,1)}, u32[]{:S(2)}) copy-start(bf16[4104,1024]{1,0:T(8,128)(2,1)} %reshape.165) | copy-start | bytes 25214980
  169.6 1.9 copy-start.2
  215.3 4.6 %copy-start.4 = (bf16[2052,512]{1,0:T(8,128)(2,1)S(1)}, bf16[2052,512]{1,0:T(8,128)(2,1)}, u32[]{:S(2)}) copy-start(bf16[2052,512]{1,0:T(8,128)(2,1)} %concatenate.18) | copy-start | bytes 6303748
  241.2 7.3 %copy-start.10 = (s32[1,128]{1,0:T(1,128)S(1)}, s32[1,128]{1,0:T(1,128)}, u32[]{:S(2)}) copy-start(s32[1,128]{1,0:T(1,128)} %param.9) | copy-start | bytes 1540
  248.4 119.8 %all-reduce.7.cloned.1.call-start = ((), (), s32[]{:S(2)}) async-start(), calls=%async_computation.1 | async-start | bytes 6291456 | tf_op jit(solution)/shard_map/psum | solution.py:101
  294.4 6.4 %copy-start.11 = (u32[32]{0:T(128)S(1)}, u32[32]{0:T(128)}, u32[]{:S(2)}) copy-start(u32[32]{0:T(128)} %constant.30) | copy-start | bytes 388
  294.4 15.2 %copy-start.7 = (f32[2048]{0:T(1024)S(1)}, f32[2048]{0:T(1024)}, u32[]{:S(2)}) copy-start(f32[2048]{0:T(1024)} %param.15) | copy-start | bytes 24580
  300.7 8.8 %copy-start.6 = (bf16[1024,768]{1,0:T(8,128)(2,1)S(1)}, bf16[1024,768]{1,0:T(8,128)(2,1)}, u32[]{:S(2)}) copy-start(bf16[1024,768]{1,0:T(8,128)(2,1)} %all-gather.3.cloned.1.call-done) | copy-start | bytes 4718596
  309.6 67.3 %copy-start.8 = (f32[2048]{0:T(1024)}, f32[2048]{0:T(1024)S(1)}, u32[]{:S(2)}) copy-start(f32[2048]{0:T(1024)S(1)} %convert_add_fusion) | copy-start | bytes 24580
Sparse Core Ops, SparseCore 0:
  248.5 45.7 all-gather.2
  300.9 67.2 all-reduce.6
where the time goes:
time: 418 us; the launch traced here: 411 us
  other arithmetic  117 us (28%)
  waiting for transfers between devices  88.3 us (21%)
  local copies, waits for them, and re-layouts  72.2 us (17%)
  matrix products  69.1 us (17%)
  blocking collectives  47.3 us (11%)
  between operations  15.3 us (4%)
    convert_element_type x6, other arithmetic, activate(): return jax.nn.gelu(norm_rows(accum), approximate=False).astype(jnp.bfloat16)  89.1 us
    psum x1, waiting for transfers between devices, local(): lax.psum(hot_sums.astype(jnp.bfloat16), 'grp').astype(jnp.float32)  58.2 us
    all_gather x1, waiting for transfers between devices, local(): accumulate_frames = lax.all_gather(frames, 'tm', axis=0, tiled=True)  26.3 us
    slice x5, local copies, waits for them, and re-layouts, odd_layer(): paired[:out_len]  23.4 us
    reshape x4, local copies, waits for them, and re-layouts, odd_layer(): jnp.concatenate([inputs, jnp.zeros((1, channels), inputs.dtype)], axis=0)  22.5 us
    dot_general x4, matrix products, odd_layer(): jnp.dot(paired[:out_len], weight[:2 * channels], preferred_element_type=j...  22.1 us
    unnamed x1, blocking collectives  21.4 us
    all_gather x1, blocking collectives, local(): labels = lax.all_gather(own_labels, 'tm', axis=0, tiled=True)  19.6 us
  transfers between devices with their start and end apart: 3, of which 3 were waited for; matrix products, arithmetic and copies ran while one was open for 1% of the time, Pallas kernels for 0%

commit v1 on v0

--- a/solution.py
+++ b/solution.py
@@ -1,12 +1,23 @@
 import jax
 import jax.numpy as jnp
 from jax import lax
+from jax.experimental import pallas as pl
+from jax.experimental.pallas import tpu as pltpu
 from jax.sharding import PartitionSpec as P
 
 HALO = 80
-
-
+STRIDE = 320
+PHASES = 64
 EPS = 1e-05
+TAIL = (
+    -0.9999932050704956,
+    -1.151200771331787,
+    -0.45877352356910706,
+    -0.05340905860066414,
+    0.008078922517597675,
+    -0.0007687128381803632,
+    3.303830453660339e-05,
+)
 
 
 def passed_along(value, axis, steps):
@@ -22,54 +33,150 @@
     return centred * lax.rsqrt(spread + EPS)
 
 
+def gelu(value):
+    size = jnp.abs(value)
+    short = jnp.minimum(size, 6.0)
+    power = jnp.float32(TAIL[-1])
+    for coefficient in TAIL[-2::-1]:
+        power = power * short + coefficient
+    return jnp.maximum(value, 0.0) - size * jnp.exp2(power)
+
+
 def activate(accum):
-    return jax.nn.gelu(norm_rows(accum), approximate=False).astype(jnp.bfloat16)
-
-
-def first_layer(samples, w_first):
-    windows = samples.reshape(-1, 5)
-    accum = jnp.dot(windows[:-1], w_first[:5], preferred_element_type=jnp.float32)
-    accum = accum + jnp.dot(windows[1:], w_first[5:], preferred_element_type=jnp.float32)
-    return activate(accum)
-
-
-def odd_layer(inputs, weight):
-    channels = inputs.shape[1]
-    out_len = (inputs.shape[0] - 3) // 2 + 1
-    paired = jnp.concatenate([inputs, jnp.zeros((1, channels), inputs.dtype)], axis=0).reshape(
-        out_len + 1, 2 * channels
-    )
-    accum = jnp.dot(paired[:out_len], weight[: 2 * channels], preferred_element_type=jnp.float32)
-    accum = accum + jnp.dot(
-        paired[1:, :channels], weight[2 * channels :], preferred_element_type=jnp.float32
-    )
-    return activate(accum)
-
-
-def even_layer(inputs, weight):
-    channels = inputs.shape[1]
-    paired = inputs.reshape(inputs.shape[0] // 2, 2 * channels)
-    return activate(jnp.dot(paired, weight, preferred_element_type=jnp.float32))
-
-
-def encode(samples, w_first, w_mid, w_tail):
-    hidden = first_layer(samples, w_first)
-    for layer_num in range(4):
-        hidden = odd_layer(hidden, w_mid[layer_num])
-    for layer_num in range(2):
-        hidden = even_layer(hidden, w_tail[layer_num])
-    return hidden
-
-
-def project(features, w_proj):
+    return gelu(norm_rows(accum)).astype(jnp.bfloat16)
+
+
+def dot(left, right):
+    return jnp.dot(left, right, preferred_element_type=jnp.float32)
+
+
+def shifted(block, following):
+    rows = block.shape[0]
+    wide = pltpu.roll(block.astype(jnp.float32), rows - 1, 0)
+    place = lax.broadcasted_iota(jnp.int32, wide.shape, 0)
+    return jnp.where(place == rows - 1, following[:1].astype(jnp.float32), wide).astype(block.dtype)
+
+
+def encoder_kernel(
+    windows, halo_windows, w_first, w_mid, w_tail, w_proj, frames,
+    even1, odd1, even2, odd2, even3, odd3, even4, odd4, even5, odd5, held_a, held_b,
+):
+    rows = windows.shape[2]
+    channels = w_first.shape[1]
+    sub = 32
+
+    def finish(held, even, odd, t):
+        for part in range(2):
+            target = (even, odd)[part]
+            for piece in range(rows // sub):
+                block = held[pl.ds(part * rows + piece * sub, sub), :]
+                target[t, pl.ds(piece * sub, sub), :] = activate(block)
+
+    def pipeline(pairs, product, even, odd):
+        if pairs <= 2:
+            for t in range(pairs):
+                held = (held_a, held_b)[t % 2]
+                held[...] = product(t)
+                finish(held, even, odd, t)
+            return
+        held_a[...] = product(0)
+
+        def body(i, carry):
+            held_b[...] = product(2 * i + 1)
+            finish(held_a, even, odd, 2 * i)
+            held_a[...] = product(jnp.minimum(2 * i + 2, pairs - 1))
+            finish(held_b, even, odd, 2 * i + 1)
+            return carry
+
+        lax.fori_loop(0, pairs // 2, body, 0)
+
+    def window_dot(block):
+        return lax.dot_general(
+            block, w_first[...], (((0,), (0,)), ((), ())), preferred_element_type=jnp.float32
+        )
+
+    pipeline(
+        PHASES // 2,
+        lambda t: jnp.concatenate([window_dot(windows[2 * t]), window_dot(windows[2 * t + 1])], axis=0),
+        even1,
+        odd1,
+    )
+    halo = activate(window_dot(halo_windows[...])).reshape(16, 16, channels)
+    layers = ((even1, odd1, even2, odd2), (even2, odd2, even3, odd3),
+              (even3, odd3, even4, odd4), (even4, odd4, even5, odd5))
+    phases = PHASES
+    need = 15
+    for layer, (even, odd, next_even, next_odd) in enumerate(layers):
+        even[phases // 2] = shifted(even[0], halo[0])
+
+        def product(t, even=even, odd=odd, layer=layer):
+            first = even[pl.ds(2 * t, 2)].reshape(2 * rows, channels)
+            second = odd[pl.ds(2 * t, 2)].reshape(2 * rows, channels)
+            third = even[pl.ds(2 * t + 1, 2)].reshape(2 * rows, channels)
+            return (
+                dot(first, w_mid[layer, 0])
+                + dot(second, w_mid[layer, 1])
+                + dot(third, w_mid[layer, 2])
+            )
+
+        pipeline(phases // 4, product, next_even, next_odd)
+        phases //= 2
+        following = (need - 3) // 2 + 1
+        if following > 0:
+            picked = [
+                jnp.concatenate([halo[2 * s + tap] for s in range(following)], axis=0) for tap in range(3)
+            ]
+            accum = dot(picked[0], w_mid[layer, 0]) + dot(picked[1], w_mid[layer, 1])
+            accum = accum + dot(picked[2], w_mid[layer, 2])
+            halo = activate(accum).reshape(following, 16, channels)
+            need = following
+    pair = dot(even5[...].reshape(2 * rows, channels), w_tail[0, 0])
+    pair = pair + dot(odd5[...].reshape(2 * rows, channels), w_tail[0, 1])
+    pair = activate(pair)
+    last = dot(pair[:rows], w_tail[1, 0]) + dot(pair[rows:], w_tail[1, 1])
+    features = activate(last)
     normed = norm_rows(features.astype(jnp.float32)).astype(jnp.bfloat16)
-    return jnp.dot(normed, w_proj, preferred_element_type=jnp.float32).astype(jnp.bfloat16)
+    frames[...] = dot(normed, w_proj[...]).astype(jnp.bfloat16)
+
+
+def encode(samples, tail_part, w_first, w_mid, w_tail, w_proj):
+    rows = samples.shape[0] // STRIDE
+    channels = w_first.shape[1]
+    grid = samples.reshape(rows, STRIDE)
+    halo_row = jnp.concatenate([tail_part, jnp.zeros((STRIDE - HALO,), samples.dtype)])[None]
+    after = jnp.concatenate([grid[1:], halo_row])[:, :HALO]
+    turned = jnp.concatenate([grid, after], axis=1).T
+    low = turned[:STRIDE].reshape(PHASES, 5, rows)
+    high = turned[5 : STRIDE + 5].reshape(PHASES, 5, rows)
+    windows = jnp.concatenate([low, high, jnp.zeros((PHASES, 6, rows), samples.dtype)], axis=1)
+    fives = tail_part.reshape(16, 5).T
+    halo_windows = jnp.concatenate(
+        [fives, jnp.concatenate([fives[:, 1:], jnp.zeros((5, 1), samples.dtype)], axis=1),
+         jnp.zeros((6, 16), samples.dtype)], axis=0)
+    halo_windows = jnp.repeat(halo_windows, 16, axis=1)
+    padded_first = jnp.concatenate([w_first, jnp.zeros((6, channels), w_first.dtype)])
+    scratch = []
+    for level in range(5):
+        half = PHASES >> (level + 1)
+        scratch.append(pltpu.VMEM((half + (level < 4), rows, channels), jnp.bfloat16))
+        scratch.append(pltpu.VMEM((half, rows, channels), jnp.bfloat16))
+    scratch += [pltpu.VMEM((2 * rows, channels), jnp.float32)] * 2
+    return pl.pallas_call(
+        encoder_kernel,
+        out_shape=jax.ShapeDtypeStruct((rows, w_proj.shape[1]), jnp.bfloat16),
+        in_specs=[pl.BlockSpec(memory_space=pltpu.VMEM)] * 6,
+        out_specs=pl.BlockSpec(memory_space=pltpu.VMEM),
+        scratch_shapes=scratch,
+        compiler_params=pltpu.CompilerParams(vmem_limit_bytes=48 * 2**20),
+        cost_estimate=pl.CostEstimate(flops=14 * 10**9, bytes_accessed=12 * 10**6, transcendentals=9 * 10**6),
+        name="encoder",
+    )(windows, halo_windows, padded_first, w_mid.reshape(4, 3, channels, channels),
+      w_tail.reshape(2, 2, channels, channels), w_proj)
 
 
 def local(wave, assign, w_first, w_mid, w_tail, w_proj, centroids, prior):
     samples = wave[0]
     tail_part = passed_along(samples[:HALO], "tm", -1)
-    features = encode(jnp.concatenate([samples, tail_part]), w_first, w_mid, w_tail)
     own_labels = assign[0]
     shard_len = centroids.shape[0]
     feat_width = centroids.shape[1]
@@ -78,7 +185,7 @@
     rounded = lax.optimization_barrier(centroids.astype(jnp.bfloat16))
     widened = rounded.astype(jnp.float32)
     centroid_sq = jnp.sum(widened * widened, axis=1)
-    frames = project(features, w_proj)
+    frames = encode(samples, tail_part, w_first, w_mid, w_tail, w_proj)
     accumulate_frames = lax.all_gather(frames, "tm", axis=0, tiled=True)
     labels = lax.all_gather(own_labels, "tm", axis=0, tiled=True)
     one_hot = labels[None, :] == centroid_ids[:, None]

time: 418 us -> 229 us (0.55); the launches traced: 411 us -> 229 us
  other arithmetic: 117 us -> 13.1 us
  local copies, waits for them, and re-layouts: 72.2 us -> 7.38 us
  matrix products: 69.1 us -> 10.5 us
  Pallas kernels: 0 us -> 47.7 us
  waiting for transfers between devices: 88.3 us -> 84.1 us
    convert_element_type x6 -> x0, other arithmetic: 89.1 us -> none  [activate(): return jax.nn.gelu(norm_rows(accum), approximate=False).astype(jnp.bfloat16)]
    dot_general x13 -> x0, matrix products: 58.7 us -> none  [the longest x4 22.1 us: odd_layer(): jnp.dot(paired[:out_len], weight[:2 * channels], preferred_element_type=j...]
    pallas_call x0 -> x1, Pallas kernels: none -> 47.7 us  [encode(): pl.pallas_call(encoder_kernel, out_shape=jax.ShapeDtypeStruct((rows, w_pr...]
    slice x7 -> x6, local copies, waits for them, and re-layouts: 33.8 us -> 1.87 us  [the longest x2 1.52 us: encode(): after = jnp.concatenate([grid[1:], halo_row])[:, :HALO]]
    reshape x6 -> x4, local copies, waits for them, and re-layouts: 22.8 us -> 0.29 us  [the longest x1 0.12 us: encode(): halo_windows = jnp.repeat(halo_windows, 16, axis=1)]
    reduce_sum x9 -> x0, other arithmetic: 14.9 us -> none  [the longest x8 14.2 us: norm_rows(): spread = jnp.mean(centred * centred, axis=-1, keepdims=True)]
    concatenate x4 -> x3, local copies, waits for them, and re-layouts: 11.8 us -> 0.81 us  [the longest x1 0.73 us: encode(): jnp.concatenate([w_first, jnp.zeros((6, channels), w_first.dtype)])]
  transfers between devices with their start and end apart: 3 -> 3, of which waited for: 3 -> 3; matrix products, arithmetic and copies ran while one was open for 1% -> 3% of each run, Pallas kernels for 0% -> 0%
where the time goes in v1:
time: 229 us
  waiting for transfers between devices  84.1 us (37%)
  blocking collectives  49.9 us (22%)
  Pallas kernels  47.7 us (21%)
  between operations  14.9 us (7%)
  other arithmetic  13.1 us (6%)
  matrix products  10.5 us (5%)
  local copies, waits for them, and re-layouts  7.38 us (3%)
    psum x1, waiting for transfers between devices, local(): lax.psum(hot_sums.astype(jnp.bfloat16), 'grp').astype(jnp.float32)  58.2 us
    pallas_call x1, Pallas kernels, encode(): pl.pallas_call(encoder_kernel, out_shape=jax.ShapeDtypeStruct((rows, w_pr...  47.7 us
    all_gather x1, waiting for transfers between devices, local(): accumulate_frames = lax.all_gather(frames, 'tm', axis=0, tiled=True)  24.6 us
    all_gather x1, blocking collectives, local(): labels = lax.all_gather(own_labels, 'tm', axis=0, tiled=True)  22.1 us
    unnamed x1, blocking collectives  21.4 us
    convert_element_type x1, other arithmetic, local(): rounded = lax.optimization_barrier(centroids.astype(jnp.bfloat16))  8.7 us
    dot_general x1, matrix products, local(): jnp.dot(one_hot.astype(jnp.bfloat16), accumulate_frames, preferred_elemen...  6.43 us
    psum x1, blocking collectives, local(): lax.psum(counts.astype(jnp.bfloat16), 'grp').astype(jnp.float32)  6.42 us
  transfers between devices with their start and end apart: 3, of which 3 were waited for; matrix products, arithmetic and copies ran while one was open for 3% of the time, Pallas kernels for 0%

profile of v1, /device:TPU:0, one launch (start us, length us, event | category | flops | bytes accessed | tf_op | source)
XLA Modules:
  0.0 229.1 jit_solution(16287442723363089362)
XLA Ops:
  7.2 0.0 all-gather.3.cloned.1.call-start
  7.2 0.7 slice_bitcast_fusion
  7.9 1.3 collective-permute-start
  9.2 1.4 slice_reduce_fusion
  10.6 1.4 reduce
  11.9 0.1 reshape_squeeze.3
  12.1 0.1 slice.25
  12.2 0.7 concatenate.27.w_first
  12.9 0.1 pad.8.clone
  13.0 1.2 collective-permute-done
  14.2 0.1 reshape.41
  14.3 0.1 copy.25
  14.4 0.1 fusion.9
  14.5 0.1 fusion.16
  14.6 0.1 copy.23
  14.8 0.1 copy.24
  15.0 0.1 copy.27
  15.1 0.1 fusion.13
  15.2 0.1 broadcast_in_dim.35
  15.3 0.1 reshape.42.halo_windows
  15.4 0.1 maximum_maximum_fusion.windows
  15.5 0.0 copy-start
  15.5 1.6 copy-done
  17.1 0.0 copy-start.1
  17.1 1.1 copy-done.1
  18.2 47.7 %encoder.1 = bf16[128,768]{1,0:T(8,128)(2,1)} custom-call(bf16[64,16,128]{2,1,0:T(8,128)(2,1)S(1)} %maximum_maximum_fusion.windows, bf16[16,256]{1,0:T(8,128)(2,1)S(1)} %reshape.42.halo_windows, bf16[16,512]{1,0:T(8,128)(2,1)S(1)} %concatenate.27.w_first, bf16[4,3,512,512]{3,2,1,0:T(8,128)(2,1)} %bitcast.21, bf16[2,2,512,512]{3,2,1,0:T(8,128)(2,1)S(1)} %bitcast.14, ...), custom_call_target="tpu_custom_call" | custom-call | flops 14000000000 | bytes 12000000 | tf_op jit(solution)/shard_map/encoder/pallas_call | solution.py:164
  65.9 0.0 all-gather.3.cloned.1.call-update
  65.9 0.2 all-reduce.6.cloned.1.call-start
  66.2 0.0 copy-done.5
  66.2 22.1 %all-gather = s32[1,1024]{1,0:T(1,128)S(1)} all-gather(s32[1,128]{1,0:T(1,128)S(1)} %copy-done.5), channel_id=2, replica_groups=mesh['grp'=4,'tm'=8] {'tm'}, dimensions={1}, use_global_device_ids=true | all-gather | bytes 4608 | tf_op jit(solution)/shard_map/all_gather | solution.py:190
  88.3 24.6 %all-gather.3.cloned.1.call-done = bf16[1024,768]{1,0:T(8,128)(2,1)} async-done(((bf16[128,768]{1,0:T(8,128)(2,1)}), bf16[1024,768]{1,0:T(8,128)(2,1)}) %all-gather.3.cloned.1.call-update) | async-done | bytes 1572880 | tf_op jit(solution)/shard_map/all_gather | solution.py:189
  112.9 6.4 %fusion.5 = bf16[2048,768]{1,0:T(8,128)(2,1)} fusion(bf16[1024,768]{1,0:T(8,128)(2,1)} %all-gather.3.cloned.1.call-done, s32[1024]{0:T(1024)S(1)} %bitcast.17, s32[2048]{0:T(1024)S(1)} %iota_add_fusion), kind=kOutput, calls=%fused_computation.9 | convolution fusion | flops 3224895488 | bytes 4730880 | tf_op jit(solution)/shard_map/dot_general | solution.py:193
  119.3 0.0 all-reduce.6.cloned.1.call-update
  119.4 0.0 copy-done.6
  119.4 0.6 dynamic-slice
  120.6 1.1 fusion.2
  121.7 6.4 %psum.15 = bf16[2048]{0:T(1024)(128)(2,1)S(1)} all-reduce(bf16[2048]{0:T(1024)(128)(2,1)S(1)} %fusion.2), channel_id=1, replica_groups=mesh['grp'=4,'tm'=8] {'grp'}, use_global_device_ids=true, to_apply=%region_2.0 | all-reduce | flops 2048 | bytes 8192 | tf_op jit(solution)/shard_map/psum | solution.py:209
  128.2 0.0 copy-done.3
  128.2 0.0 copy-done.2
  128.2 0.0 copy-start.4
  128.2 0.4 multiply_reduce_fusion.1
  128.6 58.2 %all-reduce.6.cloned.1.call-done = bf16[2048,768]{1,0:T(8,128)(2,1)} async-done(((bf16[2048,768]{1,0:T(8,128)(2,1)}), bf16[2048,768]{1,0:T(8,128)(2,1)}) %all-reduce.6.cloned.1.call-update) | async-done | bytes 3145744 | tf_op jit(solution)/shard_map/psum | solution.py:208
  186.8 8.7 %fusion.15 = (bf16[2048,768]{1,0:T(8,128)(2,1)S(1)}, f32[2048,768]{1,0:T(8,128)}) fusion(f32[2048,768]{1,0:T(8,128)} %param.14, f32[2048]{0:T(1024)S(1)} %convert_add_fusion, bf16[2048,768]{1,0:T(8,128)(2,1)} %all-reduce.6.cloned.1.call-done, f32[2048]{0:T(1024)S(1)} %copy-done.3), kind=kLoop, calls=%fused_computation.28 | loop fusion | flops 7864320 | bytes 18890752 | tf_op jit(solution)/shard_map/convert_element_type | solution.py:185
  195.5 0.0 copy-done.4
  195.5 0.7 multiply_reduce_fusion
  196.2 4.0 %select_reduce_fusion = f32[1024]{0:T(1024)S(1)} fusion(bf16[1024,768]{1,0:T(8,128)(2,1)S(1)} %copy-done.2, bf16[2048,768]{1,0:T(8,128)(2,1)S(1)} %get-tuple-element.3, f32[2048]{0:T(1024)S(1)} %multiply_reduce_fusion, s32[2048]{0:T(1024)S(1)} %iota_add_fusion, s32[1024]{0:T(1024)S(1)} %bitcast.19), kind=kOutput, calls=%fused_computation.4 | convolution fusion | flops 3231710208 | bytes 4743168 | tf_op jit(solution)/shard_map/rd,kd->rk/dot_general | solution.py:197
  200.3 21.4 %all-reduce.3 = f32[1024]{0:T(1024)S(1)} all-reduce(f32[1024]{0:T(1024)S(1)} %add_select_fusion), channel_id=3, replica_groups=mesh['grp'=4,'tm'=8] {'tm'}, use_global_device_ids=true, to_apply=%region_6.7.clone | all-reduce | flops 1024 | bytes 8192
  221.6 0.6 fusion.14
  (13 shorter events, 0.1 us)
Async XLA Ops:
  7.2 105.7 %all-gather.3.cloned.1.call-start = ((), (), s32[]{:S(2)}) async-start(), calls=%async_computation | async-start | bytes 1769472 | tf_op jit(solution)/shard_map/all_gather | solution.py:189
  7.9 6.3 %collective-permute-start = (bf16[80]{0:T(256)(128)(2,1)S(1)}, bf16[80]{0:T(256)(128)(2,1)S(1)}, u32[]{:S(2)}, u32[]{:S(2)}) collective-permute-start(bf16[80]{0:T(256)(128)(2,1)S(1)} %slice_bitcast_fusion), channel_id=1, source_target_pairs={{1,0},{2,1},{3,2},{4,3},{5,4},{6,5},{7,6},{9,8},{10,9},{11,10},{12... | collective-permute-start | bytes 488 | tf_op jit(solution)/shard_map/ppermute | solution.py:26
  15.5 1.6 copy-start
  17.1 1.1 copy-start.1
  18.2 47.9 %copy-start.5 = (s32[1,128]{1,0:T(1,128)S(1)}, s32[1,128]{1,0:T(1,128)}, u32[]{:S(2)}) copy-start(s32[1,128]{1,0:T(1,128)} %param.9) | copy-start | bytes 1540
  65.9 120.9 %all-reduce.6.cloned.1.call-start = ((), (), s32[]{:S(2)}) async-start(), calls=%async_computation.1 | async-start | bytes 6291456 | tf_op jit(solution)/shard_map/psum | solution.py:208
  112.9 6.5 %copy-start.6 = (u32[32]{0:T(128)S(1)}, u32[32]{0:T(128)}, u32[]{:S(2)}) copy-start(u32[32]{0:T(128)} %constant.29) | copy-start | bytes 388
  112.9 15.2 %copy-start.3 = (f32[2048]{0:T(1024)S(1)}, f32[2048]{0:T(1024)}, u32[]{:S(2)}) copy-start(f32[2048]{0:T(1024)} %param.15) | copy-start | bytes 24580
  112.9 15.3 %copy-start.2 = (bf16[1024,768]{1,0:T(8,128)(2,1)S(1)}, bf16[1024,768]{1,0:T(8,128)(2,1)}, u32[]{:S(2)}) copy-start(bf16[1024,768]{1,0:T(8,128)(2,1)} %all-gather.3.cloned.1.call-done) | copy-start | bytes 4718596
  128.2 67.3 %copy-start.4 = (f32[2048]{0:T(1024)}, f32[2048]{0:T(1024)S(1)}, u32[]{:S(2)}) copy-start(f32[2048]{0:T(1024)S(1)} %convert_add_fusion) | copy-start | bytes 24580
Sparse Core Ops, SparseCore 0:
  66.1 46.7 all-gather.2
  119.5 67.2 all-reduce.5

commit v2 on v1

--- a/solution.py
+++ b/solution.py
@@ -8,6 +8,8 @@
 HALO = 80
 STRIDE = 320
 PHASES = 64
+EXTRA = 16
+RADIX = 128
 EPS = 1e-05
 TAIL = (
     -0.9999932050704956,
@@ -58,7 +60,7 @@
 
 
 def encoder_kernel(
-    windows, halo_windows, w_first, w_mid, w_tail, w_proj, frames,
+    windows, halo_windows, w_first, w_mid, w_tail, w_proj, extra, frames,
     even1, odd1, even2, odd2, even3, odd3, even4, odd4, even5, odd5, held_a, held_b,
 ):
     rows = windows.shape[2]
@@ -136,10 +138,11 @@
     last = dot(pair[:rows], w_tail[1, 0]) + dot(pair[rows:], w_tail[1, 1])
     features = activate(last)
     normed = norm_rows(features.astype(jnp.float32)).astype(jnp.bfloat16)
-    frames[...] = dot(normed, w_proj[...]).astype(jnp.bfloat16)
-
-
-def encode(samples, tail_part, w_first, w_mid, w_tail, w_proj):
+    frames[:rows, :] = dot(normed, w_proj[...]).astype(jnp.bfloat16)
+    frames[rows:, :] = extra[...]
+
+
+def encode(samples, tail_part, w_first, w_mid, w_tail, w_proj, extra):
     rows = samples.shape[0] // STRIDE
     channels = w_first.shape[1]
     grid = samples.reshape(rows, STRIDE)
@@ -163,51 +166,240 @@
     scratch += [pltpu.VMEM((2 * rows, channels), jnp.float32)] * 2
     return pl.pallas_call(
         encoder_kernel,
-        out_shape=jax.ShapeDtypeStruct((rows, w_proj.shape[1]), jnp.bfloat16),
-        in_specs=[pl.BlockSpec(memory_space=pltpu.VMEM)] * 6,
+        out_shape=jax.ShapeDtypeStruct((rows + EXTRA, w_proj.shape[1]), jnp.bfloat16),
+        in_specs=[pl.BlockSpec(memory_space=pltpu.VMEM)] * 7,
         out_specs=pl.BlockSpec(memory_space=pltpu.VMEM),
         scratch_shapes=scratch,
         compiler_params=pltpu.CompilerParams(vmem_limit_bytes=48 * 2**20),
         cost_estimate=pl.CostEstimate(flops=14 * 10**9, bytes_accessed=12 * 10**6, transcendentals=9 * 10**6),
         name="encoder",
     )(windows, halo_windows, padded_first, w_mid.reshape(4, 3, channels, channels),
-      w_tail.reshape(2, 2, channels, channels), w_proj)
+      w_tail.reshape(2, 2, channels, channels), w_proj, extra)
+
+
+def remote(source, target, sent, received, device):
+    return pltpu.make_async_remote_copy(
+        src_ref=source, dst_ref=target, send_sem=sent, recv_sem=received,
+        device_id=device, device_id_type=pl.DeviceIdType.MESH,
+    )
+
+
+def gather_kernel(lines, cut, block, out, own_sem, zs, zr, xs, xr, ys, yr, cs, cr):
+    g, t = lax.axis_index("grp"), lax.axis_index("tm")
+    h, c = lax.div(g, 2), lax.rem(g, 2)
+    own, p = lax.div(t, 2), lax.rem(t, 2)
+    rows = block.shape[0]
+    over_p, over_h, over_c = (g, 2 * own + 1 - p), (2 * (1 - h) + c, t), (2 * h + 1 - c, t)
+    above, below = own < lines - 1, own > 0
+    barrier = pltpu.get_barrier_semaphore()
+    for device in (over_p, over_h, over_c):
+        pl.semaphore_signal(barrier, inc=1, device_id=device, device_id_type=pl.DeviceIdType.MESH)
+
+    @pl.when(above)
+    def _():
+        pl.semaphore_signal(barrier, inc=1, device_id=(g, t + 2), device_id_type=pl.DeviceIdType.MESH)
+
+    @pl.when(below)
+    def _():
+        pl.semaphore_signal(barrier, inc=1, device_id=(g, t - 2), device_id_type=pl.DeviceIdType.MESH)
+
+    pl.semaphore_wait(barrier, 3 + above.astype(jnp.int32) + below.astype(jnp.int32))
+
+    def slot(dh, dc, line, dp):
+        hh = h if dh == 0 else 1 - h
+        cc = c if dc == 0 else 1 - c
+        pp = p if dp == 0 else 1 - p
+        return out.at[2 * hh + cc, 2 * line + pp]
+
+    def half(ref, which):
+        return ref.at[pl.ds(0, cut), :] if which == 0 else ref.at[pl.ds(cut, rows - cut), :]
+
+    def along(way, line, source=None):
+        target = slot(0, 0, line, 0)
+        return remote(target if source is None else source, target, zs.at[way, line], zr.at[line],
+                      (g, t + 2 - 4 * way))
+
+    def to_p(kind, line, source=None):
+        target = slot(0, 0, line, 0) if kind == 0 else half(slot(1, 0, line, 0), 1)
+        return remote(target if source is None else source, target, xs.at[kind, line], xr.at[kind, line], over_p)
+
+    def to_h(kind, line, source=None):
+        target = slot(0, 0, line, 0) if kind == 0 else half(slot(0, 0, line, 1), 0)
+        return remote(target if source is None else source, target, ys.at[kind, line], yr.at[kind, line], over_h)
+
+    def to_c(dh, dp, line, source=None):
+        target = slot(dh, 0, line, dp)
+        kind = 2 * dh + dp
+        return remote(target if source is None else source, target, cs.at[kind, line], cr.at[kind, line], over_c)
+
+    def arrived(target, sent, received):
+        remote(target, target, sent, received, over_c).wait_recv()
+
+    here = pltpu.make_async_copy(block, slot(0, 0, own, 0), own_sem)
+    onward = (above, below)
+
+    def spread(line, source=None):
+        to_p(0, line, source).start()
+        to_h(0, line, source).start()
+        to_c(0, 0, line, source).start()
+
+    for way in range(2):
+        @pl.when(onward[way])
+        def _(way=way):
+            along(way, own, block).start()
+    spread(own, block)
+    here.start()
+
+    def each(step, action):
+        if step == 0:
+            action(own, 0)
+            return
+        for way in range(2):
+            line = own - step if way == 0 else own + step
+
+            @pl.when((line >= 0) & (line < lines))
+            def _(line=line, way=way):
+                action(line, way)
+
+    def first_visit(line, way):
+        arrived(slot(0, 0, line, 0), zs.at[way, line], zr.at[line])
+
+        @pl.when(onward[way])
+        def _():
+            along(way, line).start()
+
+        spread(line)
+
+    def second_visit(line, way):
+        arrived(slot(0, 0, line, 1), xs.at[0, line], xr.at[0, line])
+        to_h(1, line).start()
+        to_c(0, 1, line).start()
+        arrived(slot(1, 0, line, 0), ys.at[0, line], yr.at[0, line])
+        to_p(1, line).start()
+        to_c(1, 0, line).start()
+
+    def third_visit(line, way):
+        arrived(half(slot(1, 0, line, 1), 0), ys.at[1, line], yr.at[1, line])
+        arrived(half(slot(1, 0, line, 1), 1), xs.at[1, line], xr.at[1, line])
+        to_c(1, 1, line).start()
+
+    for step in range(1, lines):
+        each(step, first_visit)
+        each(step - 1, second_visit)
+    each(lines - 1, second_visit)
+    for step in range(lines):
+        each(step, third_visit)
+
+    def last_visit(line, way):
+        for dh in range(2):
+            for dp in range(2):
+                kind = 2 * dh + dp
+                arrived(slot(dh, 1, line, dp), cs.at[kind, line], cr.at[kind, line])
+                to_c(dh, dp, line).wait_send()
+        for kind in range(2):
+            to_p(kind, line).wait_send()
+            to_h(kind, line).wait_send()
+
+    for step in range(lines):
+        each(step, last_visit)
+    for step in range(1, lines):
+        def sent_on(line, way):
+            @pl.when(onward[way])
+            def _():
+                along(way, line).wait_send()
+
+        each(step, sent_on)
+    for way in range(2):
+        @pl.when(onward[way])
+        def _(way=way):
+            along(way, own).wait_send()
+    here.wait()
+
+
+def gather_blocks(block, groups, count):
+    lines = count // 2
+    dma = pltpu.SemaphoreType.DMA
+    return pl.pallas_call(
+        lambda *refs: gather_kernel(lines, 64, *refs),
+        out_shape=jax.ShapeDtypeStruct((groups, count) + block.shape, block.dtype),
+        in_specs=[pl.BlockSpec(memory_space=pltpu.VMEM)],
+        out_specs=pl.BlockSpec(memory_space=pl.ANY),
+        scratch_shapes=[dma, dma((2, lines)), dma((lines,)), dma((2, lines)), dma((2, lines)),
+                        dma((2, lines)), dma((2, lines)), dma((4, lines)), dma((4, lines))],
+        compiler_params=pltpu.CompilerParams(collective_id=0, has_side_effects=True, vmem_limit_bytes=4 * 2**20),
+        name="gather_blocks",
+    )(block)
+
+
+def exchange_kernel(count, terms, out, landed, sent, received):
+    g, t = lax.axis_index("grp"), lax.axis_index("tm")
+    barrier = pltpu.get_barrier_semaphore()
+    for step in range(1, count):
+        peer = lax.rem(t + step, count)
+        pl.semaphore_signal(barrier, inc=1, device_id=(g, peer), device_id_type=pl.DeviceIdType.MESH)
+    pl.semaphore_wait(barrier, count - 1)
+    copies = []
+    for step in range(1, count):
+        peer = lax.rem(t + step, count)
+        copy = remote(terms.at[peer], landed.at[step - 1], sent.at[step - 1], received.at[step - 1], (g, peer))
+        copy.start()
+        copies.append(copy)
+    total = terms[t]
+    for step in range(1, count):
+        copies[step - 1].wait()
+        total = total + landed[step - 1]
+    out[...] = total
+
+
+def exchange_terms(terms):
+    count, rows = terms.shape
+    dma = pltpu.SemaphoreType.DMA
+    return pl.pallas_call(
+        lambda *refs: exchange_kernel(count, *refs),
+        out_shape=jax.ShapeDtypeStruct((1, rows), terms.dtype),
+        in_specs=[pl.BlockSpec(memory_space=pltpu.VMEM)],
+        out_specs=pl.BlockSpec(memory_space=pltpu.VMEM),
+        scratch_shapes=[pltpu.VMEM((count - 1, 1, rows), terms.dtype), dma((count - 1,)), dma((count - 1,))],
+        compiler_params=pltpu.CompilerParams(collective_id=1, has_side_effects=True),
+        name="exchange_terms",
+    )(terms.reshape(count, 1, rows))
 
 
 def local(wave, assign, w_first, w_mid, w_tail, w_proj, centroids, prior):
     samples = wave[0]
     tail_part = passed_along(samples[:HALO], "tm", -1)
-    own_labels = assign[0]
-    shard_len = centroids.shape[0]
-    feat_width = centroids.shape[1]
+    groups, count = lax.axis_size("grp"), lax.axis_size("tm")
+    own_rows = assign.shape[1]
+    shard_len, feat_width = centroids.shape
+    digits = jnp.concatenate([assign // RADIX, assign % RADIX]).astype(jnp.bfloat16)
+    extra = jnp.pad(digits, ((0, EXTRA - 2), (0, feat_width - own_rows)))
+    block = encode(samples, tail_part, w_first, w_mid, w_tail, w_proj, extra)
+    gathered = gather_blocks(block, groups, count)
+    digits = gathered[:, :, own_rows : own_rows + 2, :own_rows].astype(jnp.int32)
+    labels = digits[:, :, 0] * RADIX + digits[:, :, 1]
+    labels = jnp.pad(labels, ((0, 0), (0, 0), (0, EXTRA)), constant_values=-1)
     first_id = lax.axis_index("tm") * shard_len
     centroid_ids = first_id + jnp.arange(shard_len, dtype=jnp.int32)
     rounded = lax.optimization_barrier(centroids.astype(jnp.bfloat16))
     widened = rounded.astype(jnp.float32)
     centroid_sq = jnp.sum(widened * widened, axis=1)
-    frames = encode(samples, tail_part, w_first, w_mid, w_tail, w_proj)
-    accumulate_frames = lax.all_gather(frames, "tm", axis=0, tiled=True)
-    labels = lax.all_gather(own_labels, "tm", axis=0, tiled=True)
-    one_hot = labels[None, :] == centroid_ids[:, None]
-    hot_rows = labels[:, None] == centroid_ids[None, :]
-    hot_sums = jnp.dot(
-        one_hot.astype(jnp.bfloat16), accumulate_frames, preferred_element_type=jnp.float32
+    one_hot = labels.reshape(1, -1) == centroid_ids[:, None]
+    total_sums = jnp.dot(
+        one_hot.astype(jnp.bfloat16), gathered.reshape(-1, feat_width), preferred_element_type=jnp.float32
     )
-    counts = jnp.sum(one_hot.astype(jnp.float32), axis=1)
-    products = jnp.einsum(
-        "rd,kd->rk", accumulate_frames, rounded, preferred_element_type=jnp.float32
-    )
-    frame_wide = accumulate_frames.astype(jnp.float32)
+    total_counts = jnp.sum(one_hot.astype(jnp.float32), axis=1)
+    group = lax.axis_index("grp")
+    sequence = lax.dynamic_index_in_dim(gathered, group, 0, keepdims=False).reshape(-1, feat_width)
+    own_labels = lax.dynamic_index_in_dim(labels, group, 0, keepdims=False).reshape(-1)
+    hot_rows = own_labels[:, None] == centroid_ids[None, :]
+    products = jnp.einsum("rd,kd->rk", sequence, rounded, preferred_element_type=jnp.float32)
+    frame_wide = sequence.astype(jnp.float32)
     squares = jnp.sum(frame_wide * frame_wide, axis=1)
-    is_owner = (labels >= first_id) & (labels < first_id + shard_len)
+    is_owner = (own_labels >= first_id) & (own_labels < first_id + shard_len)
     picked = jnp.sum(jnp.where(hot_rows, centroid_sq[None, :] - 2.0 * products, 0.0), axis=1)
     own_term = jnp.where(is_owner, squares + picked, 0.0)
-    term_sums = lax.psum_scatter(own_term, "tm", scatter_dimension=0, tiled=True)
-    distortion = (term_sums / feat_width)[None, :]
-    total_sums, total_counts = (
-        lax.psum(hot_sums.astype(jnp.bfloat16), "grp").astype(jnp.float32),
-        lax.psum(counts.astype(jnp.bfloat16), "grp").astype(jnp.float32),
-    )
+    term_sums = exchange_terms(own_term.reshape(count, -1)[:, :own_rows])
+    distortion = term_sums / feat_width
     new_counts = prior + total_counts
     new_centroids = (prior[:, None] * centroids + total_sums) / new_counts[:, None]
     return (new_centroids, new_counts, distortion)

time: 229 us -> 145 us (0.63)
  waiting for transfers between devices: 84.1 us -> 0.01 us
  blocking collectives: 49.9 us -> 0 us
  Pallas kernels: 47.7 us -> 94.3 us
  matrix products: 10.5 us -> 27.2 us
  between operations: 14.9 us -> 0.94 us
    psum x1 -> x0, waiting for transfers between devices: 58.2 us -> none  [local(): lax.psum(hot_sums.astype(jnp.bfloat16), 'grp').astype(jnp.float32)]
    pallas_call x1 -> x3, Pallas kernels: 47.7 us -> 94.3 us  [the longest x1 47.3 us: encode(): pl.pallas_call(encoder_kernel, out_shape=jax.ShapeDtypeStruct((rows + EXT...]
    all_gather x1 -> x0, waiting for transfers between devices: 24.6 us -> none  [local(): accumulate_frames = lax.all_gather(frames, 'tm', axis=0, tiled=True)]
    all_gather x1 -> x0, blocking collectives: 22.1 us -> none  [local(): labels = lax.all_gather(own_labels, 'tm', axis=0, tiled=True)]
    unnamed x1 -> x0, blocking collectives: 21.4 us -> none
    dot_general x2, matrix products: 10.5 us -> 27.2 us  [the longest x1 21.2 us: local(): jnp.dot(one_hot.astype(jnp.bfloat16), gathered.reshape(-1, feat_width), p...]
    psum x1 -> x0, blocking collectives: 6.42 us -> none  [local(): lax.psum(counts.astype(jnp.bfloat16), 'grp').astype(jnp.float32)]
    convert_element_type x1, other arithmetic: 8.7 us -> 3.24 us  [local(): rounded = lax.optimization_barrier(centroids.astype(jnp.bfloat16))]
  transfers between devices with their start and end apart: 3 -> 1, of which waited for: 3 -> 0; matrix products, arithmetic and copies ran while one was open for 3% -> 5% of each run, Pallas kernels for 0% -> 0%
where the time goes in v2:
time: 145 us
  Pallas kernels  94.3 us (65%)
  matrix products  27.2 us (19%)
  other arithmetic  13.5 us (9%)
  local copies, waits for them, and re-layouts  7.46 us (5%)
    pallas_call x1, Pallas kernels, encode(): pl.pallas_call(encoder_kernel, out_shape=jax.ShapeDtypeStruct((rows + EXT...  47.3 us
    pallas_call x1, Pallas kernels, gather_blocks(): pl.pallas_call(lambda *refs: gather_kernel(lines, 64, *refs), out_shape=j...  39.3 us
    dot_general x1, matrix products, local(): jnp.dot(one_hot.astype(jnp.bfloat16), gathered.reshape(-1, feat_width), p...  21.2 us
    pallas_call x1, Pallas kernels, exchange_terms(): pl.pallas_call(lambda *refs: exchange_kernel(count, *refs), out_shape=jax...  7.62 us
    dot_general x1, matrix products, local(): jnp.einsum('rd,kd->rk', sequence, rounded, preferred_element_type=jnp.flo...  6.01 us
    unnamed x17, local copies, waits for them, and re-layouts  3.97 us
    reduce_sum x1, other arithmetic, local(): total_counts = jnp.sum(one_hot.astype(jnp.float32), axis=1)  3.81 us
    convert_element_type x1, other arithmetic, local(): rounded = lax.optimization_barrier(centroids.astype(jnp.bfloat16))  3.24 us
  transfers between devices with their start and end apart: 1, of which 0 were waited for; matrix products, arithmetic and copies ran while one was open for 5% of the time, Pallas kernels for 0%

profile of v2, /device:TPU:0, one launch (start us, length us, event | category | flops | bytes accessed | tf_op | source)
XLA Modules:
  0.0 144.6 jit_solution(6535065657830432284)
XLA Ops:
  0.6 0.7 slice_bitcast_fusion
  1.3 1.3 collective-permute-start
  2.6 1.4 slice_reduce_fusion
  4.0 1.4 reduce.1
  5.4 0.1 reshape_squeeze.3
  5.5 0.1 slice.37
  5.6 0.7 fusion.22
  6.3 0.0 copy-start.1
  6.3 0.0 copy-start.2
  6.3 3.2 %convert_element_type.23 = bf16[2048,768]{1,0:T(8,128)(2,1)S(1)} convert(f32[2048,768]{1,0:T(8,128)} %param.14) | non-fusion elementwise | flops 1572864 | bytes 9437184 | tf_op jit(solution)/shard_map/convert_element_type | solution.py:383
  9.6 0.0 copy-start.3
  9.6 0.7 multiply_reduce_fusion
  10.3 1.0 copy-done.3
  11.2 0.0 copy-done.5
  11.3 0.1 pad.20.clone
  11.4 0.0 collective-permute-done
  11.4 0.1 reshape.69
  11.5 0.1 copy.23
  11.6 0.1 fusion.8
  11.7 0.1 fusion.23
  11.8 0.1 copy.21
  12.0 0.1 copy.22
  12.1 0.1 copy.27
  12.2 0.1 fusion.19
  12.3 0.1 broadcast_in_dim.30
  12.4 0.1 reshape.70.halo_windows
  12.5 0.1 maximum_maximum_fusion.windows
  12.7 0.0 copy-done.1
  12.7 0.0 copy-done.2
  12.7 47.3 %encoder.1.refs_0_ = bf16[144,768]{1,0:T(8,128)(2,1)S(1)} custom-call(bf16[64,16,128]{2,1,0:T(8,128)(2,1)S(1)} %maximum_maximum_fusion.windows, bf16[16,256]{1,0:T(8,128)(2,1)S(1)} %reshape.70.halo_windows, bf16[16,512]{1,0:T(8,128)(2,1)S(1)} %concatenate.31.w_first, bf16[4,3,512,512]{3,2,1,0:T(8,128)(2,1)} %bitcast.23, ...), custom_call_target="tpu_custom_call" | custom-call | flops 14000000000 | bytes 12000000 | tf_op jit(solution)/shard_map/encoder/pallas_call | solution.py:167
  60.0 0.0 copy-start.4
  60.0 39.3 %gather_blocks.1 = bf16[4,8,144,768]{3,2,1,0:T(8,128)(2,1)S(1)} custom-call(bf16[144,768]{1,0:T(8,128)(2,1)S(1)} %encoder.1.refs_0_), custom_call_target="tpu_custom_call" | custom-call | tf_op jit(solution)/shard_map/gather_blocks/pallas_call | solution.py:322
  99.4 0.0 copy-start
  99.4 2.9 %copy-done = bf16[4,8,144,768]{3,2,1,0:T(8,128)(2,1)} copy-done((bf16[4,8,144,768]{3,2,1,0:T(8,128)(2,1)}, bf16[4,8,144,768]{3,2,1,0:T(8,128)(2,1)S(1)}, u32[]{:S(2)}) %copy-start) | copy-done | bytes 7077912
  102.3 1.6 %multiply_reduce_fusion.1 = (f32[8,144]{1,0:T(8,128)S(1)}, bf16[1,8,144,768]{3,2,1,0:T(8,128)(2,1)}) fusion(bf16[4,8,144,768]{3,2,1,0:T(8,128)(2,1)S(1)} %gather_blocks.1, s32[]{:T(128)S(6)} %select_n.29), kind=kLoop, calls=%fused_computation.10 | loop fusion | flops 2653056 | bytes 3543556 | tf_op jit(solution)/shard_map/reduce_sum | solution.py:397
  103.9 0.1 eq.36
  104.0 0.0 copy-done.4
  104.0 0.0 copy-start.6
  104.0 6.0 %select_reduce_fusion = f32[1152]{0:T(1024)S(1)} fusion(bf16[1152,768]{1,0:T(8,128)(2,1)} %bitcast.19, bf16[2048,768]{1,0:T(8,128)(2,1)S(1)} %copy-done.4, f32[2048]{0:T(1024)S(1)} %multiply_reduce_fusion, s32[2048]{0:T(1024)S(1)} %iota_add_fusion, s32[1152]{0:T(1024)S(1)} %eq.36), kind=kOutput, calls=%fused_computation.7 | convolution fusion | flops 3635674112 | bytes 4940800 | tf_op jit(solution)/shard_map/rd,kd->rk/dot_general | solution.py:395
  110.0 0.1 reduce_sum.42
  110.1 0.6 fusion.20
  110.7 7.6 %exchange_terms.1 = f32[1,128]{1,0:T(1,128)} custom-call(f32[8,1,128]{2,1,0:T(1,128)} %bitcast.22), custom_call_target="tpu_custom_call" | custom-call | tf_op jit(solution)/shard_map/exchange_terms/pallas_call | solution.py:357
  118.4 1.1 broadcast_multiply_fusion
  119.5 0.1 eq.32
  119.6 3.8 %fusion.2 = f32[2048]{0:T(1024)S(1)} fusion(s32[4608]{0:T(1024)S(1)} %eq.32, s32[2048]{0:T(1024)S(1)} %iota_add_fusion), kind=kLoop, calls=%fused_computation.3 | loop fusion | flops 28309504 | bytes 34816 | tf_op jit(solution)/shard_map/reduce_sum | solution.py:390
  123.4 0.0 copy-start.7
  123.4 21.2 %add_divide_fusion = f32[2048,768]{1,0:T(8,128)} fusion(f32[2048,768]{1,0:T(8,128)} %param.14, bf16[4608,768]{1,0:T(8,128)(2,1)} %bitcast.17, s32[4608]{0:T(1024)S(1)} %eq.32, s32[2048]{0:T(1024)S(1)} %iota_add_fusion, f32[2048]{0:T(1024)S(1)} %add.62, f32[2048]{0:T(1024)S(1)} %copy-done.6), kind=kOutput, calls=%fused_computation.9 | convolution fusion | flops 14509670400 | bytes 19703808 | tf_op jit(solution)/shard_map/dot_general | solution.py:387
  144.6 0.0 copy-done.7
  (17 shorter events, 0.2 us)
Async XLA Ops:
  1.3 10.1 %collective-permute-start = (bf16[80]{0:T(256)(128)(2,1)S(1)}, bf16[80]{0:T(256)(128)(2,1)S(1)}, u32[]{:S(2)}, u32[]{:S(2)}) collective-permute-start(bf16[80]{0:T(256)(128)(2,1)S(1)} %slice_bitcast_fusion), channel_id=1, source_target_pairs={{1,0},{2,1},{3,2},{4,3},{5,4},{6,5},{7,6},{9,8},{10,9},{11,10},{12... | collective-permute-start | bytes 488 | tf_op jit(solution)/shard_map/ppermute | solution.py:28
  6.3 5.0 %copy-start.5 = (bf16[10,512]{1,0:T(8,128)(2,1)S(1)}, bf16[10,512]{1,0:T(8,128)(2,1)}, u32[]{:S(2)}) copy-start(bf16[10,512]{1,0:T(8,128)(2,1)} %param.10) | copy-start | bytes 30724
  6.3 6.4 %copy-start.1 = (bf16[2,1024,512]{2,1,0:T(8,128)(2,1)S(1)}, bf16[2,1024,512]{2,1,0:T(8,128)(2,1)}, u32[]{:S(2)}) copy-start(bf16[2,1024,512]{2,1,0:T(8,128)(2,1)} %param.12) | copy-start | bytes 6291460
  6.3 6.4 %copy-start.2 = (bf16[512,768]{1,0:T(8,128)(2,1)S(1)}, bf16[512,768]{1,0:T(8,128)(2,1)}, u32[]{:S(2)}) copy-start(bf16[512,768]{1,0:T(8,128)(2,1)} %w_proj.1) | copy-start | bytes 2359300
  9.6 1.7 %copy-start.3 = (bf16[2048,768]{1,0:T(8,128)(2,1)}, bf16[2048,768]{1,0:T(8,128)(2,1)S(1)}, u32[]{:S(2)}) copy-start(bf16[2048,768]{1,0:T(8,128)(2,1)S(1)} %convert_element_type.23) | copy-start | bytes 9437188
  60.0 44.0 %copy-start.4 = (bf16[2048,768]{1,0:T(8,128)(2,1)S(1)}, bf16[2048,768]{1,0:T(8,128)(2,1)}, u32[]{:S(2)}) copy-start(bf16[2048,768]{1,0:T(8,128)(2,1)} %copy-done.3) | copy-start | bytes 9437188
  99.4 2.9 %copy-start = (bf16[4,8,144,768]{3,2,1,0:T(8,128)(2,1)}, bf16[4,8,144,768]{3,2,1,0:T(8,128)(2,1)S(1)}, u32[]{:S(2)}) copy-start(bf16[4,8,144,768]{3,2,1,0:T(8,128)(2,1)S(1)} %gather_blocks.1) | copy-start | bytes 21233668
  104.0 19.4 %copy-start.6 = (f32[2048]{0:T(1024)S(1)}, f32[2048]{0:T(1024)}, u32[]{:S(2)}) copy-start(f32[2048]{0:T(1024)} %param.15) | copy-start | bytes 24580
  123.4 21.2 %copy-start.7 = (f32[2048]{0:T(1024)}, f32[2048]{0:T(1024)S(1)}, u32[]{:S(2)}) copy-start(f32[2048]{0:T(1024)S(1)} %add.62) | copy-start | bytes 24580

commit v3 on v2

--- a/solution.py
+++ b/solution.py
@@ -184,7 +184,10 @@
     )
 
 
-def gather_kernel(lines, cut, block, out, own_sem, zs, zr, xs, xr, ys, yr, cs, cr):
+def gather_kernel(
+    lines, cut, block, centroids, sums, counts, term, out, rounded, squares, terms, landed,
+    own_sem, zs, zr, xs, xr, ys, yr, cs, cr, ts, tr,
+):
     g, t = lax.axis_index("grp"), lax.axis_index("tm")
     h, c = lax.div(g, 2), lax.rem(g, 2)
     own, p = lax.div(t, 2), lax.rem(t, 2)
@@ -192,18 +195,11 @@
     over_p, over_h, over_c = (g, 2 * own + 1 - p), (2 * (1 - h) + c, t), (2 * h + 1 - c, t)
     above, below = own < lines - 1, own > 0
     barrier = pltpu.get_barrier_semaphore()
-    for device in (over_p, over_h, over_c):
+    devices = 2 * lines
+    peers = [(g, lax.rem(t + step, devices)) for step in range(1, devices)]
+    for device in peers + [over_h, over_c]:
         pl.semaphore_signal(barrier, inc=1, device_id=device, device_id_type=pl.DeviceIdType.MESH)
-
-    @pl.when(above)
-    def _():
-        pl.semaphore_signal(barrier, inc=1, device_id=(g, t + 2), device_id_type=pl.DeviceIdType.MESH)
-
-    @pl.when(below)
-    def _():
-        pl.semaphore_signal(barrier, inc=1, device_id=(g, t - 2), device_id_type=pl.DeviceIdType.MESH)
-
-    pl.semaphore_wait(barrier, 3 + above.astype(jnp.int32) + below.astype(jnp.int32))
+    pl.semaphore_wait(barrier, devices + 1)
 
     def slot(dh, dc, line, dp):
         hh = h if dh == 0 else 1 - h
@@ -283,18 +279,119 @@
         arrived(half(slot(1, 0, line, 1), 1), xs.at[1, line], xr.at[1, line])
         to_c(1, 1, line).start()
 
+    shard, width = centroids.shape
+    frame_rows = counts.shape[1]
+    tile = 256
+    first_id = t * shard
+
+    def prepare(i, carry):
+        held = pl.ds(pl.multiple_of(i * tile, tile), tile)
+        short = centroids[held, :].astype(jnp.bfloat16)
+        rounded[held, :] = short
+        wide = short.astype(jnp.float32)
+        squares[held, :] = jnp.broadcast_to(jnp.sum(wide * wide, axis=1, keepdims=True), (tile, frame_rows))
+        sums[held, :] = jnp.zeros((tile, width), jnp.float32)
+        counts[held, :] = jnp.zeros((tile, frame_rows), jnp.float32)
+        return carry
+
+    lax.fori_loop(0, shard // tile, prepare, 0)
+
+    def accumulate(dh, dc, line, scored):
+        group = 2 * (h if dh == 0 else 1 - h) + (c if dc == 0 else 1 - c)
+        pair = [out[group, 2 * line + k, pl.ds(0, frame_rows), :] for k in range(2)]
+        pair = jnp.concatenate(pair, axis=0)
+        labels = []
+        for k in range(2):
+            digits = out[group, 2 * line + k, pl.ds(frame_rows, EXTRA), pl.ds(0, frame_rows)].astype(jnp.float32)
+            labels.append(digits[0:1] * float(RADIX) + digits[1:2])
+        labels = jnp.concatenate(labels, axis=1)
+
+        def one(i, picked):
+            held = pl.ds(pl.multiple_of(i * tile, tile), tile)
+            ids = lax.broadcasted_iota(jnp.int32, (tile, 2 * frame_rows), 0) + (first_id + i * tile)
+            hot = ids.astype(jnp.float32) == labels
+            ones = jnp.where(hot, 1.0, 0.0)
+            sums[held, :] += dot(ones.astype(jnp.bfloat16), pair)
+            counts[held, :] += ones[:, :frame_rows] + ones[:, frame_rows:]
+            if not scored:
+                return picked
+            products = lax.dot_general(
+                rounded[held, :], pair, (((1,), (1,)), ((), ())), preferred_element_type=jnp.float32
+            )
+            value = jnp.where(hot, squares[held, :][:, :1] - 2.0 * products, 0.0)
+            return picked + jnp.sum(value, axis=0, keepdims=True)
+
+        picked = lax.fori_loop(0, shard // tile, one, jnp.zeros((1, 2 * frame_rows), jnp.float32))
+        if scored:
+            terms[2 * line] = picked[:, :frame_rows]
+            terms[2 * line + 1] = picked[:, frame_rows:]
+
+    def each_rolled(step, action):
+        if step < 0 or step >= lines:
+            return
+        if step == 0:
+            action(own)
+            return
+
+        def body(way, carry):
+            line = own - step + 2 * step * way
+
+            @pl.when((line >= 0) & (line < lines))
+            def _():
+                action(line)
+
+            return carry
+
+        lax.fori_loop(0, 2, body, 0)
+
+    def to_peer(peer):
+        return remote(terms.at[peer], landed.at[t], ts.at[peer], tr.at[t], (g, peer))
+
+    def compute_0(line):
+        accumulate(0, 0, line, True)
+
+    def compute_1(line):
+        for dp in range(2):
+            arrived(slot(0, 1, line, dp), cs.at[dp, line], cr.at[dp, line])
+        for k in range(2):
+            @pl.when(2 * line + k != t)
+            def _(k=k):
+                to_peer(2 * line + k).start()
+
+        accumulate(0, 1, line, False)
+
+    def compute_2(line):
+        accumulate(1, 0, line, False)
+
+    def compute_3(line):
+        for dp in range(2):
+            arrived(slot(1, 1, line, dp), cs.at[2 + dp, line], cr.at[2 + dp, line])
+        accumulate(1, 1, line, False)
+
     for step in range(1, lines):
         each(step, first_visit)
         each(step - 1, second_visit)
+        if step == 1:
+            here.wait()
+        each_rolled(step - 1, compute_0)
+        each_rolled(step - 2, compute_1)
     each(lines - 1, second_visit)
+    each_rolled(lines - 1, compute_0)
+    each(0, third_visit)
+    each_rolled(lines - 2, compute_1)
     for step in range(lines):
-        each(step, third_visit)
+        if step + 1 < lines:
+            each(step + 1, third_visit)
+        each_rolled(step, compute_2)
+        if step == 0:
+            each_rolled(lines - 1, compute_1)
+        each_rolled(step - 1, compute_3)
+    each_rolled(lines - 1, compute_3)
 
     def last_visit(line, way):
         for dh in range(2):
             for dp in range(2):
                 kind = 2 * dh + dp
-                arrived(slot(dh, 1, line, dp), cs.at[kind, line], cr.at[kind, line])
                 to_c(dh, dp, line).wait_send()
         for kind in range(2):
             to_p(kind, line).wait_send()
@@ -313,56 +410,51 @@
         @pl.when(onward[way])
         def _(way=way):
             along(way, own).wait_send()
-    here.wait()
-
-
-def gather_blocks(block, groups, count):
+    landed[t] = terms[t]
+
+    def settle(peer, carry):
+        @pl.when(peer != t)
+        def _():
+            to_peer(peer).wait_send()
+            arrived_term = remote(landed.at[peer], landed.at[peer], ts.at[peer], tr.at[peer], over_c)
+            arrived_term.wait_recv()
+
+        return carry
+
+    lax.fori_loop(0, devices, settle, 0)
+    total = landed[0]
+    for peer in range(1, devices):
+        total = total + landed[peer]
+    term[...] = total
+
+
+def gather_and_sum(block, centroids, groups, count, frame_rows):
     lines = count // 2
+    shard, width = centroids.shape
     dma = pltpu.SemaphoreType.DMA
+    vmem = pl.BlockSpec(memory_space=pltpu.VMEM)
     return pl.pallas_call(
         lambda *refs: gather_kernel(lines, 64, *refs),
-        out_shape=jax.ShapeDtypeStruct((groups, count) + block.shape, block.dtype),
-        in_specs=[pl.BlockSpec(memory_space=pltpu.VMEM)],
-        out_specs=pl.BlockSpec(memory_space=pl.ANY),
-        scratch_shapes=[dma, dma((2, lines)), dma((lines,)), dma((2, lines)), dma((2, lines)),
-                        dma((2, lines)), dma((2, lines)), dma((4, lines)), dma((4, lines))],
-        compiler_params=pltpu.CompilerParams(collective_id=0, has_side_effects=True, vmem_limit_bytes=4 * 2**20),
-        name="gather_blocks",
-    )(block)
-
-
-def exchange_kernel(count, terms, out, landed, sent, received):
-    g, t = lax.axis_index("grp"), lax.axis_index("tm")
-    barrier = pltpu.get_barrier_semaphore()
-    for step in range(1, count):
-        peer = lax.rem(t + step, count)
-        pl.semaphore_signal(barrier, inc=1, device_id=(g, peer), device_id_type=pl.DeviceIdType.MESH)
-    pl.semaphore_wait(barrier, count - 1)
-    copies = []
-    for step in range(1, count):
-        peer = lax.rem(t + step, count)
-        copy = remote(terms.at[peer], landed.at[step - 1], sent.at[step - 1], received.at[step - 1], (g, peer))
-        copy.start()
-        copies.append(copy)
-    total = terms[t]
-    for step in range(1, count):
-        copies[step - 1].wait()
-        total = total + landed[step - 1]
-    out[...] = total
-
-
-def exchange_terms(terms):
-    count, rows = terms.shape
-    dma = pltpu.SemaphoreType.DMA
-    return pl.pallas_call(
-        lambda *refs: exchange_kernel(count, *refs),
-        out_shape=jax.ShapeDtypeStruct((1, rows), terms.dtype),
-        in_specs=[pl.BlockSpec(memory_space=pltpu.VMEM)],
-        out_specs=pl.BlockSpec(memory_space=pltpu.VMEM),
-        scratch_shapes=[pltpu.VMEM((count - 1, 1, rows), terms.dtype), dma((count - 1,)), dma((count - 1,))],
-        compiler_params=pltpu.CompilerParams(collective_id=1, has_side_effects=True),
-        name="exchange_terms",
-    )(terms.reshape(count, 1, rows))
+        out_shape=(
+            jax.ShapeDtypeStruct((shard, width), jnp.float32),
+            jax.ShapeDtypeStruct((shard, frame_rows), jnp.float32),
+            jax.ShapeDtypeStruct((1, frame_rows), jnp.float32),
+        ),
+        in_specs=[vmem, vmem],
+        out_specs=(vmem, vmem, vmem),
+        scratch_shapes=[
+            pltpu.VMEM((groups, count) + block.shape, block.dtype),
+            pltpu.VMEM((shard, width), jnp.bfloat16),
+            pltpu.VMEM((shard, frame_rows), jnp.float32),
+            pltpu.VMEM((count, 1, frame_rows), jnp.float32),
+            pltpu.VMEM((count, 1, frame_rows), jnp.float32),
+            dma, dma((2, lines)), dma((lines,)), dma((2, lines)), dma((2, lines)),
+            dma((2, lines)), dma((2, lines)), dma((4, lines)), dma((4, lines)),
+            dma((count,)), dma((count,)),
+        ],
+        compiler_params=pltpu.CompilerParams(collective_id=0, has_side_effects=True, vmem_limit_bytes=50 * 2**20),
+        name="gather_and_sum",
+    )(block, centroids)
 
 
 def local(wave, assign, w_first, w_mid, w_tail, w_proj, centroids, prior):
@@ -370,36 +462,15 @@
     tail_part = passed_along(samples[:HALO], "tm", -1)
     groups, count = lax.axis_size("grp"), lax.axis_size("tm")
     own_rows = assign.shape[1]
-    shard_len, feat_width = centroids.shape
+    feat_width = centroids.shape[1]
     digits = jnp.concatenate([assign // RADIX, assign % RADIX]).astype(jnp.bfloat16)
     extra = jnp.pad(digits, ((0, EXTRA - 2), (0, feat_width - own_rows)))
     block = encode(samples, tail_part, w_first, w_mid, w_tail, w_proj, extra)
-    gathered = gather_blocks(block, groups, count)
-    digits = gathered[:, :, own_rows : own_rows + 2, :own_rows].astype(jnp.int32)
-    labels = digits[:, :, 0] * RADIX + digits[:, :, 1]
-    labels = jnp.pad(labels, ((0, 0), (0, 0), (0, EXTRA)), constant_values=-1)
-    first_id = lax.axis_index("tm") * shard_len
-    centroid_ids = first_id + jnp.arange(shard_len, dtype=jnp.int32)
-    rounded = lax.optimization_barrier(centroids.astype(jnp.bfloat16))
-    widened = rounded.astype(jnp.float32)
-    centroid_sq = jnp.sum(widened * widened, axis=1)
-    one_hot = labels.reshape(1, -1) == centroid_ids[:, None]
-    total_sums = jnp.dot(
-        one_hot.astype(jnp.bfloat16), gathered.reshape(-1, feat_width), preferred_element_type=jnp.float32
-    )
-    total_counts = jnp.sum(one_hot.astype(jnp.float32), axis=1)
-    group = lax.axis_index("grp")
-    sequence = lax.dynamic_index_in_dim(gathered, group, 0, keepdims=False).reshape(-1, feat_width)
-    own_labels = lax.dynamic_index_in_dim(labels, group, 0, keepdims=False).reshape(-1)
-    hot_rows = own_labels[:, None] == centroid_ids[None, :]
-    products = jnp.einsum("rd,kd->rk", sequence, rounded, preferred_element_type=jnp.float32)
-    frame_wide = sequence.astype(jnp.float32)
-    squares = jnp.sum(frame_wide * frame_wide, axis=1)
-    is_owner = (own_labels >= first_id) & (own_labels < first_id + shard_len)
-    picked = jnp.sum(jnp.where(hot_rows, centroid_sq[None, :] - 2.0 * products, 0.0), axis=1)
-    own_term = jnp.where(is_owner, squares + picked, 0.0)
-    term_sums = exchange_terms(own_term.reshape(count, -1)[:, :own_rows])
-    distortion = term_sums / feat_width
+    total_sums, lane_counts, term = gather_and_sum(block, centroids, groups, count, own_rows)
+    own_frames = block[:own_rows].astype(jnp.float32)
+    squares = jnp.sum(own_frames * own_frames, axis=1)
+    distortion = (squares[None, :] + term) / feat_width
+    total_counts = jnp.sum(lane_counts, axis=1)
     new_counts = prior + total_counts
     new_centroids = (prior[:, None] * centroids + total_sums) / new_counts[:, None]
     return (new_centroids, new_counts, distortion)

time: 145 us -> 136 us (0.938)
  matrix products: 27.2 us -> 0 us
  Pallas kernels: 94.3 us -> 115 us
  other arithmetic: 13.5 us -> 10.9 us
    dot_general x2 -> x0, matrix products: 27.2 us -> none  [the longest x1 21.2 us: local(): jnp.dot(one_hot.astype(jnp.bfloat16), gathered.reshape(-1, feat_width), p...]
    pallas_call x2 -> x1, Pallas kernels: 46.9 us -> 67.7 us  [gather_and_sum(): pl.pallas_call(lambda *refs: gather_kernel(lines, 64, *refs), out_shape=(...]
    div x1 -> x2, other arithmetic: 1.14 us -> 8.15 us  [the longest x1 7.63 us: local(): (prior[:, None] * centroids + total_sums) / new_counts[:, None]]
    reduce_sum x3 -> x2, other arithmetic: 6.14 us -> 0.46 us  [the longest x1 0.34 us: local(): total_counts = jnp.sum(lane_counts, axis=1)]
    convert_element_type x2 -> x0, other arithmetic: 3.25 us -> none  [the longest x1 3.24 us: local(): rounded = lax.optimization_barrier(centroids.astype(jnp.bfloat16))]
    unnamed x17 -> x9, local copies, waits for them, and re-layouts: 3.97 us -> 2.84 us
  transfers between devices with their start and end apart: 1 -> 1, of which waited for: 0 -> 1; matrix products, arithmetic and copies ran while one was open for 5% -> 3% of each run, Pallas kernels for 0% -> 0%
where the time goes in v3:
time: 136 us; the launch traced here: 135 us
  Pallas kernels  115 us (85%)
  other arithmetic  10.9 us (8%)
  local copies, waits for them, and re-layouts  6.79 us (5%)
    pallas_call x1, Pallas kernels, gather_and_sum(): pl.pallas_call(lambda *refs: gather_kernel(lines, 64, *refs), out_shape=(...  67.7 us
    pallas_call x1, Pallas kernels, encode(): pl.pallas_call(encoder_kernel, out_shape=jax.ShapeDtypeStruct((rows + EXT...  47 us
    div x1, other arithmetic, local(): (prior[:, None] * centroids + total_sums) / new_counts[:, None]  7.63 us
    unnamed x9, local copies, waits for them, and re-layouts  2.84 us
  transfers between devices with their start and end apart: 1, of which 1 were waited for; matrix products, arithmetic and copies ran while one was open for 3% of the time, Pallas kernels for 0%

profile of v3, /device:TPU:0, one launch (start us, length us, event | category | flops | bytes accessed | tf_op | source)
XLA Modules:
  0.0 135.0 jit_solution(3653578589747017615)
XLA Ops:
  0.6 0.7 slice_bitcast_fusion
  1.3 1.3 collective-permute-start
  2.6 1.4 %slice_reduce_fusion = bf16[40640]{0:T(1024)(128)(2,1)S(1)} fusion(bf16[1,40960]{1,0:T(2,128)(2,1)} %param.8), kind=kLoop, calls=%fused_computation.3 | loop fusion | bytes 162560 | tf_op jit(solution)/shard_map/slice | solution.py:150
  4.0 0.7 fusion.14
  4.7 1.4 %reduce = bf16[40960]{0:T(1024)(128)(2,1)S(1)} reduce(bf16[1,40960]{1,0:T(2,128)(2,1)} %param.8, bf16[]{:T(256)} %constant.51), dimensions={0}, to_apply=%param.8.reduce_sub_computation | reduce | bytes 163842 | tf_op args[0]
  6.0 0.1 reshape_squeeze.3
  6.1 0.1 slice.28
  6.3 0.7 concatenate.31.w_first
  7.0 0.1 pad.15.clone
  7.1 0.5 collective-permute-done
  7.6 0.1 reshape.30
  7.7 0.1 copy.17
  7.9 0.1 copy.19
  8.0 0.1 fusion.11
  8.0 0.1 broadcast_in_dim.22
  8.1 0.1 reshape.31.halo_windows
  8.3 0.1 fusion.1
  8.4 0.1 fusion.15
  8.5 0.1 copy.15
  8.6 0.1 copy.16
  8.8 0.1 maximum_maximum_fusion.windows
  8.9 0.0 copy-start
  9.0 1.6 %copy-done = bf16[2,1024,512]{2,1,0:T(8,128)(2,1)S(1)} copy-done((bf16[2,1024,512]{2,1,0:T(8,128)(2,1)S(1)}, bf16[2,1024,512]{2,1,0:T(8,128)(2,1)}, u32[]{:S(2)}) %copy-start) | copy-done | bytes 2097176
  10.5 0.0 copy-start.1
  10.5 1.1 copy-done.1
  11.7 47.0 %encoder.1.refs_0_ = bf16[144,768]{1,0:T(8,128)(2,1)S(1)} custom-call(bf16[64,16,128]{2,1,0:T(8,128)(2,1)S(1)} %maximum_maximum_fusion.windows, bf16[16,256]{1,0:T(8,128)(2,1)S(1)} %reshape.31.halo_windows, bf16[16,512]{1,0:T(8,128)(2,1)S(1)} %concatenate.31.w_first, bf16[4,3,512,512]{3,2,1,0:T(8,128)(2,1)} %bitcast.14, ...), custom_call_target="tpu_custom_call" | custom-call | flops 14000000000 | bytes 12000000 | tf_op jit(solution)/shard_map/encoder/pallas_call | solution.py:167
  58.7 0.0 copy-start.2
  58.7 0.1 multiply_reduce_fusion
  58.8 67.7 %gather_and_sum.1 = (f32[2048,768]{1,0:T(8,128)}, f32[2048,128]{1,0:T(8,128)S(1)}, f32[1,128]{1,0:T(1,128)S(1)}) custom-call(bf16[144,768]{1,0:T(8,128)(2,1)S(1)} %encoder.1.refs_0_, f32[2048,768]{1,0:T(8,128)} %refs_1_.1), custom_call_target="tpu_custom_call" | custom-call | tf_op jit(solution)/shard_map/gather_and_sum/pallas_call | solution.py:436
  126.5 0.5 fusion.13
  127.0 0.3 reduce_sum.18
  127.3 0.0 copy-done.2
  127.3 0.0 copy-start.3
  127.4 7.6 %add_divide_fusion = f32[2048,768]{1,0:T(8,128)} fusion(f32[2048,768]{1,0:T(8,128)} %get-tuple-element.6, f32[2048,768]{1,0:T(8,128)} %refs_1_.1, f32[2048]{0:T(1024)S(1)} %add.26, f32[2048]{0:T(1024)S(1)} %copy-done.2), kind=kLoop, calls=%fused_computation | loop fusion | flops 4718592 | bytes 18890752 | tf_op jit(solution)/shard_map/div | solution.py:475
  135.0 0.0 copy-done.3
  (8 shorter events, 0.1 us)
Async XLA Ops:
  1.3 6.3 %collective-permute-start = (bf16[80]{0:T(256)(128)(2,1)S(1)}, bf16[80]{0:T(256)(128)(2,1)S(1)}, u32[]{:S(2)}, u32[]{:S(2)}) collective-permute-start(bf16[80]{0:T(256)(128)(2,1)S(1)} %slice_bitcast_fusion), channel_id=1, source_target_pairs={{1,0},{2,1},{3,2},{4,3},{5,4},{6,5},{7,6},{9,8},{10,9},{11,10},{12... | collective-permute-start | bytes 488 | tf_op jit(solution)/shard_map/ppermute | solution.py:28
  8.9 1.6 %copy-start = (bf16[2,1024,512]{2,1,0:T(8,128)(2,1)S(1)}, bf16[2,1024,512]{2,1,0:T(8,128)(2,1)}, u32[]{:S(2)}) copy-start(bf16[2,1024,512]{2,1,0:T(8,128)(2,1)} %param.12) | copy-start | bytes 6291460
  10.5 1.1 copy-start.1
  58.7 68.7 %copy-start.2 = (f32[2048]{0:T(1024)S(1)}, f32[2048]{0:T(1024)}, u32[]{:S(2)}) copy-start(f32[2048]{0:T(1024)} %param.15) | copy-start | bytes 24580
  127.3 7.6 %copy-start.3 = (f32[2048]{0:T(1024)}, f32[2048]{0:T(1024)S(1)}, u32[]{:S(2)}) copy-start(f32[2048]{0:T(1024)S(1)} %add.26) | copy-start | bytes 24580

commit v4 on v3

--- a/solution.py
+++ b/solution.py
@@ -281,7 +281,7 @@
 
     shard, width = centroids.shape
     frame_rows = counts.shape[1]
-    tile = 256
+    tile = min(512, shard)
     first_id = t * shard
 
     def prepare(i, carry):

time: 136 us -> 128 us (0.941)
  Pallas kernels: 115 us -> 108 us
    pallas_call x1, Pallas kernels: 67.7 us -> 60.6 us  [gather_and_sum(): pl.pallas_call(lambda *refs: gather_kernel(lines, 64, *refs), out_shape=(...]
  transfers between devices with their start and end apart: 1 -> 1, of which waited for: 1 -> 1; matrix products, arithmetic and copies ran while one was open for 3% -> 4% of each run, Pallas kernels for 0% -> 0%
where the time goes in v4:
time: 128 us
  Pallas kernels  108 us (84%)
  other arithmetic  10.9 us (9%)
  local copies, waits for them, and re-layouts  6.79 us (5%)
  starting transfers between devices  1.28 us (1%)
    pallas_call x1, Pallas kernels, gather_and_sum(): pl.pallas_call(lambda *refs: gather_kernel(lines, 64, *refs), out_shape=(...  60.6 us
    pallas_call x1, Pallas kernels, encode(): pl.pallas_call(encoder_kernel, out_shape=jax.ShapeDtypeStruct((rows + EXT...  47 us
    div x1, other arithmetic, local(): (prior[:, None] * centroids + total_sums) / new_counts[:, None]  7.63 us
    unnamed x9, local copies, waits for them, and re-layouts  2.84 us
  transfers between devices with their start and end apart: 1, of which 1 were waited for; matrix products, arithmetic and copies ran while one was open for 4% of the time, Pallas kernels for 0%

profile of v4, /device:TPU:0, one launch (start us, length us, event | category | flops | bytes accessed | tf_op | source)
XLA Modules:
  0.0 127.9 jit_solution(7686778502647652083)
XLA Ops:
  0.6 0.7 slice_bitcast_fusion
  1.3 1.3 %collective-permute-start = (bf16[80]{0:T(256)(128)(2,1)S(1)}, bf16[80]{0:T(256)(128)(2,1)S(1)}, u32[]{:S(2)}, u32[]{:S(2)}) collective-permute-start(bf16[80]{0:T(256)(128)(2,1)S(1)} %slice_bitcast_fusion), channel_id=1, source_target_pairs={{1,0},{2,1},{3,2},{4,3},{5,4},{6,5},{7,6},{9,8},{10,9},{11,10},{12... | collective-permute-start | bytes 488 | tf_op jit(solution)/shard_map/ppermute | solution.py:28
  2.6 1.4 %slice_reduce_fusion = bf16[40640]{0:T(1024)(128)(2,1)S(1)} fusion(bf16[1,40960]{1,0:T(2,128)(2,1)} %param.8), kind=kLoop, calls=%fused_computation.3 | loop fusion | bytes 162560 | tf_op jit(solution)/shard_map/slice | solution.py:150
  4.0 0.7 fusion.14
  4.7 1.4 %reduce = bf16[40960]{0:T(1024)(128)(2,1)S(1)} reduce(bf16[1,40960]{1,0:T(2,128)(2,1)} %param.8, bf16[]{:T(256)} %constant.51), dimensions={0}, to_apply=%param.8.reduce_sub_computation | reduce | bytes 163842 | tf_op args[0]
  6.0 0.1 reshape_squeeze.3
  6.1 0.1 slice.28
  6.3 0.7 concatenate.31.w_first
  7.0 0.1 pad.15.clone
  7.1 0.5 collective-permute-done
  7.6 0.1 reshape.30
  7.7 0.1 copy.17
  7.9 0.1 copy.19
  8.0 0.1 fusion.11
  8.0 0.1 broadcast_in_dim.22
  8.1 0.1 reshape.31.halo_windows
  8.3 0.1 fusion.1
  8.4 0.1 fusion.15
  8.5 0.1 copy.15
  8.6 0.1 copy.16
  8.8 0.1 maximum_maximum_fusion.windows
  8.9 0.0 copy-start
  9.0 1.6 %copy-done = bf16[2,1024,512]{2,1,0:T(8,128)(2,1)S(1)} copy-done((bf16[2,1024,512]{2,1,0:T(8,128)(2,1)S(1)}, bf16[2,1024,512]{2,1,0:T(8,128)(2,1)}, u32[]{:S(2)}) %copy-start) | copy-done | bytes 2097176
  10.5 0.0 copy-start.1
  10.5 1.1 copy-done.1
  11.7 47.0 %encoder.1.refs_0_ = bf16[144,768]{1,0:T(8,128)(2,1)S(1)} custom-call(bf16[64,16,128]{2,1,0:T(8,128)(2,1)S(1)} %maximum_maximum_fusion.windows, bf16[16,256]{1,0:T(8,128)(2,1)S(1)} %reshape.31.halo_windows, bf16[16,512]{1,0:T(8,128)(2,1)S(1)} %concatenate.31.w_first, bf16[4,3,512,512]{3,2,1,0:T(8,128)(2,1)} %bitcast.14, ...), custom_call_target="tpu_custom_call" | custom-call | flops 14000000000 | bytes 12000000 | tf_op jit(solution)/shard_map/encoder/pallas_call | solution.py:167
  58.7 0.0 copy-start.2
  58.7 0.1 multiply_reduce_fusion
  58.8 60.6 %gather_and_sum.1 = (f32[2048,768]{1,0:T(8,128)}, f32[2048,128]{1,0:T(8,128)S(1)}, f32[1,128]{1,0:T(1,128)S(1)}) custom-call(bf16[144,768]{1,0:T(8,128)(2,1)S(1)} %encoder.1.refs_0_, f32[2048,768]{1,0:T(8,128)} %refs_1_.1), custom_call_target="tpu_custom_call" | custom-call | tf_op jit(solution)/shard_map/gather_and_sum/pallas_call | solution.py:436
  119.4 0.5 fusion.13
  119.9 0.3 reduce_sum.18
  120.2 0.0 copy-done.2
  120.3 0.0 copy-start.3
  120.3 7.6 %add_divide_fusion = f32[2048,768]{1,0:T(8,128)} fusion(f32[2048,768]{1,0:T(8,128)} %get-tuple-element.6, f32[2048,768]{1,0:T(8,128)} %refs_1_.1, f32[2048]{0:T(1024)S(1)} %add.26, f32[2048]{0:T(1024)S(1)} %copy-done.2), kind=kLoop, calls=%fused_computation | loop fusion | flops 4718592 | bytes 18890752 | tf_op jit(solution)/shard_map/div | solution.py:475
  127.9 0.0 copy-done.3
  (8 shorter events, 0.1 us)
Async XLA Ops:
  1.3 6.3 %collective-permute-start = (bf16[80]{0:T(256)(128)(2,1)S(1)}, bf16[80]{0:T(256)(128)(2,1)S(1)}, u32[]{:S(2)}, u32[]{:S(2)}) collective-permute-start(bf16[80]{0:T(256)(128)(2,1)S(1)} %slice_bitcast_fusion), channel_id=1, source_target_pairs={{1,0},{2,1},{3,2},{4,3},{5,4},{6,5},{7,6},{9,8},{10,9},{11,10},{12... | collective-permute-start | bytes 488 | tf_op jit(solution)/shard_map/ppermute | solution.py:28
  8.9 1.6 %copy-start = (bf16[2,1024,512]{2,1,0:T(8,128)(2,1)S(1)}, bf16[2,1024,512]{2,1,0:T(8,128)(2,1)}, u32[]{:S(2)}) copy-start(bf16[2,1024,512]{2,1,0:T(8,128)(2,1)} %param.12) | copy-start | bytes 6291460
  10.5 1.1 copy-start.1
  58.7 61.6 %copy-start.2 = (f32[2048]{0:T(1024)S(1)}, f32[2048]{0:T(1024)}, u32[]{:S(2)}) copy-start(f32[2048]{0:T(1024)} %param.15) | copy-start | bytes 24580
  120.3 7.6 %copy-start.3 = (f32[2048]{0:T(1024)}, f32[2048]{0:T(1024)S(1)}, u32[]{:S(2)}) copy-start(f32[2048]{0:T(1024)S(1)} %add.26) | copy-start | bytes 24580
